TPU v7x, 768 devices: a whole 4x8x12 slice. The times are simulated.
768 devices in a mesh: pts: 192 (over z, x_lo, y), ctr: 4 (over x_hi, core).
Axes of the slice: x: 4 (x_hi: 2, x_lo: 2; x = x_hi * 2 + x_lo), y: 8, z: 12, core: 2. Of those that a mesh axis runs over, the one named last changes fastest.
Arguments:
- points: bfloat16 [32, 393216], P(None, 'pts'), may hold values from -6 to 6
- centres: bfloat16 [32, 32768], P(None, 'ctr'), may hold values from -6 to 6
- coef: float32 [16, 32768], P(None, 'ctr'), may hold values from -6 to 6
- resid: float32 [16, 32768], P(None, 'ctr'), may hold values from -6 to 6
- direction: float32 [16, 32768], P(None, 'ctr'), may hold values from -6 to 6
- precond: float32 [32768], P('ctr'), may hold values from 0.5 to 4
Outputs:
- coef_next: float32 [16, 32768], P(None, 'ctr')
- resid_next: float32 [16, 32768], P(None, 'ctr')
- dir_next: float32 [16, 32768], P(None, 'ctr')
All inputs are finite; a program needn't handle non-finite values.
Results may differ from a plain program's by a relative error of at most 0.0012.
Values may be sent and summed in bfloat16 or wider, within the bound.
A program may use at most 128 MiB of HBM per device.

v0:
```python
import functools

import jax
import jax.numpy as jnp
from jax import lax
from jax.sharding import Mesh
from jax.sharding import PartitionSpec as P

CTR = ("ctr_0", "ctr_1")
PTS = ("pts_0", "pts_1", "pts_2")
PTS_CTR = ("pts_0", "pts_1", "pts_2", "ctr_0", "ctr_1")


def gathered_total(x, axis):
    blocks = lax.all_gather(x, axis).astype(jnp.float32)
    return blocks.sum(axis=0)


def sum_in_order(blocks, axes, sequence):
    inside = blocks.shape[1:]
    blocks = blocks.reshape(*(lax.axis_size(a) for a in axes), *inside)
    blocks = jnp.moveaxis(blocks, sequence, range(len(axes))).reshape(-1, *inside)
    for k in sequence:
        blocks = lax.psum_scatter(blocks, axes[k], scatter_dimension=0, tiled=True)
    return blocks[0]


def in_blocks(x, dim, peers):
    before, after = (x.shape[:dim], x.shape[dim + 1 :])
    return jnp.moveaxis(x.reshape(*before, peers, -1, *after), dim, 0)


def summed_rows(x, axes, sequence, dim):
    peers = lax.axis_size(axes)
    return sum_in_order(in_blocks(x, dim, peers), axes, sequence)


def over_axes(x, axes):
    return functools.reduce(lax.psum, axes, x)


def joined_along(blocks, dim):
    blocks = jnp.moveaxis(blocks, 0, dim)
    shape = blocks.shape
    return blocks.reshape(*shape[:dim], shape[dim] * shape[dim + 1], *shape[dim + 2 :])


def gather_in_order(x, axes, sequence):
    blocks = x
    for k in sequence:
        blocks = lax.all_gather(blocks, axes[k])
    done = sequence[::-1]
    back = [done.index(k) for k in range(len(axes))]
    blocks = blocks.transpose(*back, *range(len(axes), blocks.ndim))
    return blocks.reshape(-1, *x.shape)


def gathered_by_axis(x, axes, sequence, dim):
    return joined_along(gather_in_order(x, axes, sequence), dim)


def build_kernel(points, centres):
    cent32 = centres.astype(jnp.float32)
    csq = jnp.sum(cent32 * cent32, axis=0)
    feat = points.shape[0]
    rows = points.shape[1]
    width = min(256, rows)
    count = rows // width
    pieces = points.reshape(feat, count, width).transpose(1, 0, 2)

    def one_block(block):
        pts32 = block.astype(jnp.float32)
        xsq = jnp.sum(pts32 * pts32, axis=0)
        cross = lax.dot_general(
            block, centres, (((0,), (0,)), ((), ())), preferred_element_type=jnp.float32
        )
        return jnp.exp(-0.125 * (xsq[:, None] + csq[None, :] - 2.0 * cross)).astype(jnp.bfloat16)

    tiles = lax.map(one_block, pieces)
    return tiles.reshape(rows, centres.shape[1])


def shards(points, centres, coef, resid, direction, precond):
    kern = build_kernel(points, centres)
    dirb = direction.astype(jnp.bfloat16)
    fit_part = lax.dot_general(
        dirb, kern, (((1,), (1,)), ((), ())), preferred_element_type=jnp.float32
    )
    fitted = gathered_total(fit_part.astype(jnp.bfloat16), CTR).astype(jnp.float32)
    col_part = jnp.dot(fitted.astype(jnp.bfloat16), kern, preferred_element_type=jnp.float32)
    num_pts = lax.axis_size(PTS)
    scale = 2048.0 / (points.shape[1] * num_pts)
    ctr_dev = centres.shape[1]
    share = (ctr_dev + num_pts - 1) // num_pts
    extra = share * num_pts - ctr_dev
    padded = jnp.pad(col_part, ((0, 0), (0, extra)))
    col_share = summed_rows(padded, PTS, (0, 2, 1), 1)
    start = lax.axis_index(PTS) * share

    def take(vector):
        wide = jnp.pad(vector, ((0, 0), (0, extra)))
        return lax.dynamic_slice_in_dim(wide, start, share, 1)

    dir_s = take(direction)
    coef_s = take(coef)
    resid_s = take(resid)
    prec_s = take(precond[None, :])
    image = col_share * scale + 0.5 * dir_s
    rz_part = jnp.sum(resid_s * resid_s * prec_s, axis=1)
    curv, rz = (over_axes(jnp.sum(dir_s * image, axis=1), PTS_CTR), over_axes(rz_part, PTS_CTR))
    alpha = rz / curv
    coef_new = coef_s + alpha[:, None] * dir_s
    resid_new = resid_s - alpha[:, None] * image
    scaled = prec_s * resid_new
    rz_new = over_axes(jnp.sum(resid_new * scaled, axis=1), PTS_CTR)
    dir_new = scaled + (rz_new / rz)[:, None] * dir_s
    stacked = jnp.stack([coef_new, resid_new, dir_new])
    gathered = gathered_by_axis(stacked, PTS, (1, 0, 2), 2)[:, :, :ctr_dev]
    return (gathered[0], gathered[1], gathered[2])


def solution(mesh):
    finer = Mesh(
        mesh.devices.reshape(12, 2, 8, 2, 2), ("pts_0", "pts_1", "pts_2", "ctr_0", "ctr_1")
    )
    in_specs = (P(None, PTS), P(None, CTR), P(None, CTR), P(None, CTR), P(None, CTR), P(CTR))
    out_specs = (P(None, CTR), P(None, CTR), P(None, CTR))
    return jax.shard_map(
        shards, mesh=finer, in_specs=in_specs, out_specs=out_specs, check_vma=False
    )
```

profile of v0, /device:TPU:1, one launch (start us, length us, event | category | flops | bytes accessed | tf_op | source)
XLA Modules:
  0.0 441.7 jit_solution(6254024149651982379)
XLA Ops:
  7.2 0.0 reduce-scatter.4.cloned.1.call-start
  7.2 0.9 copy.20
  8.2 1.2 multiply_reduce_fusion.1
  9.4 0.0 copy-start
  9.4 42.5 %while.10 = (s32[]{:T(128)}, bf16[8,256,8192]{2,1,0:T(8,128)(2,1)}, bf16[8,32,256]{2,1,0:T(8,128)(2,1)S(1)}, f32[8192]{0:T(1024)S(1)}, bf16[32,8192]{1,0:T(8,128)(2,1)}, /*index=5*/s32[]{:T(128)}) while((s32[]{:T(128)}, bf16[8,256,8192]{2,1,0:T(8,128)(2,1)}, bf16[8,32,256]{2,1,0:T(8,128)(2,1)S(1)}, f32[8192]{0:T(1024)S(1)}, ...), condition=%wide.region_9.10_spmd, body=%wide.region_7.9_spmd.sunk | while | flops 144727808 | bytes 4787273 | solution.py:79
  9.4 5.3 %fusion.26 = bf16[8,256,8192]{2,1,0:T(8,128)(2,1)} fusion(bf16[8,256,8192]{2,1,0:T(8,128)(2,1)} %get-tuple-element.114, s32[]{:T(128)} %get-tuple-element.113, bf16[32,8192]{1,0:T(8,128)(2,1)} %get-tuple-element.123, f32[8192]{0:T(1024)S(1)} %get-tuple-element.122, f32[256]{0:T(256)S(1)} %multiply_reduce_fusion.5, ...), kind=kOutput, calls=%fused_computation.6.clone.1 | convolution fusion | flops 144703488 | bytes 4769792 | tf_op jit(solution)/shard_map/while/body/eval_jaxpr/dot_general | solution.py:74
  14.8 5.3 %fusion.26 = bf16[8,256,8192]{2,1,0:T(8,128)(2,1)} fusion(bf16[8,256,8192]{2,1,0:T(8,128)(2,1)} %get-tuple-element.114, s32[]{:T(128)} %get-tuple-element.113, bf16[32,8192]{1,0:T(8,128)(2,1)} %get-tuple-element.123, f32[8192]{0:T(1024)S(1)} %get-tuple-element.122, f32[256]{0:T(256)S(1)} %multiply_reduce_fusion.5, ...), kind=kOutput, calls=%fused_computation.6.clone.1 | convolution fusion | flops 144703488 | bytes 4769792 | tf_op jit(solution)/shard_map/while/body/eval_jaxpr/dot_general | solution.py:74
  20.1 5.3 %fusion.26 = bf16[8,256,8192]{2,1,0:T(8,128)(2,1)} fusion(bf16[8,256,8192]{2,1,0:T(8,128)(2,1)} %get-tuple-element.114, s32[]{:T(128)} %get-tuple-element.113, bf16[32,8192]{1,0:T(8,128)(2,1)} %get-tuple-element.123, f32[8192]{0:T(1024)S(1)} %get-tuple-element.122, f32[256]{0:T(256)S(1)} %multiply_reduce_fusion.5, ...), kind=kOutput, calls=%fused_computation.6.clone.1 | convolution fusion | flops 144703488 | bytes 4769792 | tf_op jit(solution)/shard_map/while/body/eval_jaxpr/dot_general | solution.py:74
  25.4 5.3 %fusion.26 = bf16[8,256,8192]{2,1,0:T(8,128)(2,1)} fusion(bf16[8,256,8192]{2,1,0:T(8,128)(2,1)} %get-tuple-element.114, s32[]{:T(128)} %get-tuple-element.113, bf16[32,8192]{1,0:T(8,128)(2,1)} %get-tuple-element.123, f32[8192]{0:T(1024)S(1)} %get-tuple-element.122, f32[256]{0:T(256)S(1)} %multiply_reduce_fusion.5, ...), kind=kOutput, calls=%fused_computation.6.clone.1 | convolution fusion | flops 144703488 | bytes 4769792 | tf_op jit(solution)/shard_map/while/body/eval_jaxpr/dot_general | solution.py:74
  30.7 5.2 %fusion.26 = bf16[8,256,8192]{2,1,0:T(8,128)(2,1)} fusion(bf16[8,256,8192]{2,1,0:T(8,128)(2,1)} %get-tuple-element.114, s32[]{:T(128)} %get-tuple-element.113, bf16[32,8192]{1,0:T(8,128)(2,1)} %get-tuple-element.123, f32[8192]{0:T(1024)S(1)} %get-tuple-element.122, f32[256]{0:T(256)S(1)} %multiply_reduce_fusion.5, ...), kind=kOutput, calls=%fused_computation.6.clone.1 | convolution fusion | flops 144703488 | bytes 4769792 | tf_op jit(solution)/shard_map/while/body/eval_jaxpr/dot_general | solution.py:74
  36.0 5.3 %fusion.26 = bf16[8,256,8192]{2,1,0:T(8,128)(2,1)} fusion(bf16[8,256,8192]{2,1,0:T(8,128)(2,1)} %get-tuple-element.114, s32[]{:T(128)} %get-tuple-element.113, bf16[32,8192]{1,0:T(8,128)(2,1)} %get-tuple-element.123, f32[8192]{0:T(1024)S(1)} %get-tuple-element.122, f32[256]{0:T(256)S(1)} %multiply_reduce_fusion.5, ...), kind=kOutput, calls=%fused_computation.6.clone.1 | convolution fusion | flops 144703488 | bytes 4769792 | tf_op jit(solution)/shard_map/while/body/eval_jaxpr/dot_general | solution.py:74
  41.3 5.3 %fusion.26 = bf16[8,256,8192]{2,1,0:T(8,128)(2,1)} fusion(bf16[8,256,8192]{2,1,0:T(8,128)(2,1)} %get-tuple-element.114, s32[]{:T(128)} %get-tuple-element.113, bf16[32,8192]{1,0:T(8,128)(2,1)} %get-tuple-element.123, f32[8192]{0:T(1024)S(1)} %get-tuple-element.122, f32[256]{0:T(256)S(1)} %multiply_reduce_fusion.5, ...), kind=kOutput, calls=%fused_computation.6.clone.1 | convolution fusion | flops 144703488 | bytes 4769792 | tf_op jit(solution)/shard_map/while/body/eval_jaxpr/dot_general | solution.py:74
  46.6 5.3 %fusion.26 = bf16[8,256,8192]{2,1,0:T(8,128)(2,1)} fusion(bf16[8,256,8192]{2,1,0:T(8,128)(2,1)} %get-tuple-element.114, s32[]{:T(128)} %get-tuple-element.113, bf16[32,8192]{1,0:T(8,128)(2,1)} %get-tuple-element.123, f32[8192]{0:T(1024)S(1)} %get-tuple-element.122, f32[256]{0:T(256)S(1)} %multiply_reduce_fusion.5, ...), kind=kOutput, calls=%fused_computation.6.clone.1 | convolution fusion | flops 144703488 | bytes 4769792 | tf_op jit(solution)/shard_map/while/body/eval_jaxpr/dot_general | solution.py:74
  51.9 0.0 copy-done
  51.9 15.0 %fusion.9 = bf16[16,2048]{1,0:T(8,128)(2,1)S(1)} fusion(bf16[2048,8192]{1,0:T(8,128)(2,1)} %bitcast.65, f32[16,8192]{1,0:T(8,128)S(1)} %copy-done), kind=kOutput, calls=%fused_computation.12 | convolution fusion | flops 537034752 | bytes 34144256 | tf_op jit(solution)/shard_map/dot_general | solution.py:86
  66.9 17.6 %all-gather = bf16[64,2048]{1,0:T(8,128)(2,1)S(1)} all-gather(bf16[16,2048]{1,0:T(8,128)(2,1)S(1)} %fusion.9), channel_id=2, replica_groups=mesh['pts_0'=12,'pts_1'=2,'pts_2'=8,'ctr_0'=2,'ctr_1'=2] {'ctr_0','ctr_1'}, dimensions={0}, use_global_device_ids=true | all-gather | bytes 327680 | tf_op jit(solution)/shard_map/all_gather | solution.py:15
  84.6 0.0 copy-start.2
  84.6 12.8 %fusion.16 = f32[16,8192]{1,0:T(8,128)S(1)} fusion(bf16[16,2048]{1,0:T(8,128)(2,1)S(1)} %reduce_sum.59, bf16[2048,8192]{1,0:T(8,128)(2,1)} %bitcast.66), kind=kOutput, calls=%fused_computation.34 | convolution fusion | flops 536870912 | bytes 34144256 | tf_op jit(solution)/shard_map/dot_general | solution.py:90
  97.4 0.0 copy-start.1
  97.5 1.9 reshape.35
  99.4 2.1 copy.17
  101.5 0.0 reduce-scatter.4.cloned.1.call-update
  101.5 0.0 reduce-scatter.6.cloned.1.call-start
  101.6 49.8 %reduce-scatter.4.cloned.1.call-done = f32[16,16,43]{2,1,0:T(8,128)} async-done(((f32[192,16,43]{2,1,0:T(8,128)}), f32[16,16,43]{2,1,0:T(8,128)}) %reduce-scatter.4.cloned.1.call-update) | async-done | bytes 44048 | tf_op jit(solution)/shard_map/reduce_scatter | solution.py:24
  151.4 0.0 reduce-scatter.6.cloned.1.call-update
  151.4 0.0 reduce-scatter.8.cloned.1.call-start
  151.5 0.0 copy-done.2
  151.5 0.1 fusion.15
  151.6 44.8 %reduce-scatter.6.cloned.1.call-done = f32[2,16,43]{2,1,0:T(8,128)} async-done(((f32[16,16,43]{2,1,0:T(8,128)}), f32[2,16,43]{2,1,0:T(8,128)}) %reduce-scatter.6.cloned.1.call-update) | async-done | bytes 5520 | tf_op jit(solution)/shard_map/reduce_scatter | solution.py:24
  196.4 0.0 reduce-scatter.8.cloned.1.call-update
  196.4 0.0 all-gather.6.cloned.1.call-start
  196.4 0.0 copy-done.1
  196.5 0.2 multiply_reduce_fusion.3
  196.6 27.0 %reduce-scatter.8.cloned.1.call-done = f32[1,16,43]{2,1,0:T(8,128)} async-done(((f32[2,16,43]{2,1,0:T(8,128)}), f32[1,16,43]{2,1,0:T(8,128)}) %reduce-scatter.8.cloned.1.call-update) | async-done | bytes 2768 | tf_op jit(solution)/shard_map/reduce_scatter | solution.py:24
  223.6 0.9 multiply_reduce_fusion.2
  224.5 19.9 %all-reduce.5 = (f32[16]{0:T(128)S(1)}, f32[16]{0:T(128)S(1)}) all-reduce(f32[16]{0:T(128)S(1)} %get-tuple-element.70, f32[16]{0:T(128)S(1)} %get-tuple-element.68), channel_id=1, replica_groups=mesh['pts_0'=12,'pts_1'=2,'pts_2'=8,'ctr_0'=2,'ctr_1'=2] {'pts_0'}, use_global_device_ids=true, to_apply=%region_1.2 | all-reduce | flops 32 | bytes 256 | tf_op jit(solution)/shard_map/psum | solution.py:39
  244.4 3.8 all-reduce.9
  248.2 13.2 %all-reduce.6 = (f32[16]{0:T(128)S(1)}, f32[16]{0:T(128)S(1)}) all-reduce(f32[16]{0:T(128)S(1)} %get-tuple-element.64, f32[16]{0:T(128)S(1)} %get-tuple-element.65), channel_id=1, replica_groups=mesh['pts_0'=12,'pts_1'=2,'pts_2'=8,'ctr_0'=2,'ctr_1'=2] {'pts_2'}, use_global_device_ids=true, to_apply=%region_3.4 | all-reduce | flops 32 | bytes 256 | tf_op jit(solution)/shard_map/psum | solution.py:39
  261.4 5.5 %all-reduce.8 = (f32[16]{0:T(128)S(1)}, f32[16]{0:T(128)S(1)}) all-reduce(f32[16]{0:T(128)S(1)} %get-tuple-element.58, f32[16]{0:T(128)S(1)} %get-tuple-element.59), channel_id=1, replica_groups=mesh['pts_0'=12,'pts_1'=2,'pts_2'=8,'ctr_0'=2,'ctr_1'=2] {'ctr_0'}, use_global_device_ids=true, to_apply=%region_4.5 | all-reduce | flops 32 | bytes 256 | tf_op jit(solution)/shard_map/psum | solution.py:39
  266.9 14.7 %all-reduce.7 = (f32[16]{0:T(128)S(1)}, f32[16]{0:T(128)S(1)}) all-reduce(f32[16]{0:T(128)S(1)} %get-tuple-element.62, f32[16]{0:T(128)S(1)} %get-tuple-element.63), channel_id=1, replica_groups=mesh['pts_0'=12,'pts_1'=2,'pts_2'=8,'ctr_0'=2,'ctr_1'=2] {'ctr_1'}, use_global_device_ids=true, to_apply=%region_5.6 | all-reduce | flops 32 | bytes 256 | tf_op jit(solution)/shard_map/psum | solution.py:39
  281.6 0.9 fusion.12
  282.5 15.7 %psum.115 = f32[16]{0:T(128)S(1)} all-reduce(f32[16]{0:T(128)S(1)} %get-tuple-element.66), channel_id=1, replica_groups=mesh['pts_0'=12,'pts_1'=2,'pts_2'=8,'ctr_0'=2,'ctr_1'=2] {'pts_0'}, use_global_device_ids=true, to_apply=%region_21.22 | all-reduce | flops 16 | bytes 128 | tf_op jit(solution)/shard_map/psum | solution.py:39
  298.2 3.8 psum.116
  302.0 11.6 %psum.117 = f32[16]{0:T(128)S(1)} all-reduce(f32[16]{0:T(128)S(1)} %psum.116), channel_id=1, replica_groups=mesh['pts_0'=12,'pts_1'=2,'pts_2'=8,'ctr_0'=2,'ctr_1'=2] {'pts_2'}, use_global_device_ids=true, to_apply=%region_23.24 | all-reduce | flops 16 | bytes 128 | tf_op jit(solution)/shard_map/psum | solution.py:39
  313.6 5.3 %psum.118 = f32[16]{0:T(128)S(1)} all-reduce(f32[16]{0:T(128)S(1)} %psum.117), channel_id=1, replica_groups=mesh['pts_0'=12,'pts_1'=2,'pts_2'=8,'ctr_0'=2,'ctr_1'=2] {'ctr_0'}, use_global_device_ids=true, to_apply=%region_24.25 | all-reduce | flops 16 | bytes 128 | tf_op jit(solution)/shard_map/psum | solution.py:39
  318.9 13.9 %psum.119 = f32[16]{0:T(128)S(1)} all-reduce(f32[16]{0:T(128)S(1)} %psum.118), channel_id=1, replica_groups=mesh['pts_0'=12,'pts_1'=2,'pts_2'=8,'ctr_0'=2,'ctr_1'=2] {'ctr_1'}, use_global_device_ids=true, to_apply=%region_25.26 | all-reduce | flops 16 | bytes 128 | tf_op jit(solution)/shard_map/psum | solution.py:39
  332.8 0.1 fusion.13
  332.8 3.4 all-gather.1
  336.2 21.6 %all-gather.2 = f32[24,3,16,43]{3,2,1,0:T(8,128)} all-gather(f32[2,3,16,43]{3,2,1,0:T(8,128)S(1)} %bitcast.74), channel_id=4, replica_groups=mesh['pts_0'=12,'pts_1'=2,'pts_2'=8,'ctr_0'=2,'ctr_1'=2] {'pts_0'}, dimensions={0}, use_global_device_ids=true | all-gather | bytes 214656 | tf_op jit(solution)/shard_map/all_gather | solution.py:51
  357.8 0.0 all-gather.6.cloned.1.call-update
  357.8 65.4 %all-gather.6.cloned.1.call-done = f32[96,2,3,16,43]{4,3,2,1,0:T(8,128)} async-done(((f32[12,2,3,16,43]{4,3,2,1,0:T(8,128)}), f32[96,2,3,16,43]{4,3,2,1,0:T(8,128)}) %all-gather.6.cloned.1.call-update) | async-done | bytes 1585168 | tf_op jit(solution)/shard_map/all_gather | solution.py:51
  423.2 2.9 copy.18
  426.1 3.5 copy.19
  429.7 4.3 reshape.39
  434.0 1.2 slice_bitcast_fusion
  (15 shorter events, 0.3 us)
Async XLA Ops:
  7.2 144.3 %reduce-scatter.4.cloned.1.call-start = ((), (), s32[]{:S(2)}) async-start(), calls=%async_computation.3 | async-start | bytes 1703936 | tf_op jit(solution)/shard_map/reduce_scatter | solution.py:24
  9.4 42.5 %copy-start = (f32[16,8192]{1,0:T(8,128)S(1)}, f32[16,8192]{1,0:T(8,128)}, u32[]{:S(2)}) copy-start(f32[16,8192]{1,0:T(8,128)} %param.12) | copy-start | bytes 1572868
  84.6 66.9 %copy-start.2 = (f32[8192]{0:T(1024)S(1)}, f32[8192]{0:T(1024)}, u32[]{:S(2)}) copy-start(f32[8192]{0:T(1024)} %param.13) | copy-start | bytes 98308
  97.4 99.0 %copy-start.1 = (f32[16,8192]{1,0:T(8,128)S(1)}, f32[16,8192]{1,0:T(8,128)}, u32[]{:S(2)}) copy-start(f32[16,8192]{1,0:T(8,128)} %param.11) | copy-start | bytes 1572868
  101.5 94.9 %reduce-scatter.6.cloned.1.call-start = ((), (), s32[]{:S(2)}) async-start(), calls=%async_computation.4 | async-start | bytes 147456 | tf_op jit(solution)/shard_map/reduce_scatter | solution.py:24
  151.4 72.2 %reduce-scatter.8.cloned.1.call-start = ((), (), s32[]{:S(2)}) async-start(), calls=%async_computation.5 | async-start | bytes 24576 | tf_op jit(solution)/shard_map/reduce_scatter | solution.py:24
  196.4 226.8 %all-gather.6.cloned.1.call-start = ((), (), s32[]{:S(2)}) async-start(), calls=%async_computation.6 | async-start | bytes 5308416 | tf_op jit(solution)/shard_map/all_gather | solution.py:51
Sparse Core Ops, SparseCore 0:
  101.6 49.7 reduce-scatter.3
  154.5 41.8 reduce-scatter.5
  199.7 23.9 reduce-scatter.7
  358.0 65.1 all-gather.5
where the time goes:
time: 443 us; the launch traced here: 442 us
  waiting for transfers between devices  187 us (42%)
  blocking collectives  150 us (34%)
  matrix products  70.1 us (16%)
  local copies, waits for them, and re-layouts  17 us (4%)
  between operations  13.9 us (3%)
    reduce_scatter x3, waiting for transfers between devices, sum_in_order(): blocks = lax.psum_scatter(blocks, axes[k], scatter_dimension=0, tiled=True)  122 us
    psum x10, blocking collectives, over_axes(): return functools.reduce(lax.psum, axes, x)  107 us
    all_gather x1, waiting for transfers between devices, gather_in_order(): blocks = lax.all_gather(blocks, axes[k])  65.4 us
    dot_general x8, matrix products, one_block(): lax.dot_general(block, centres, (((0,), (0,)), ((), ())), preferred_eleme...  42.3 us
    all_gather x2, blocking collectives, gather_in_order(): blocks = lax.all_gather(blocks, axes[k])  25 us
    all_gather x1, blocking collectives, gathered_total(): blocks = lax.all_gather(x, axis).astype(jnp.float32)  17.6 us
    dot_general x1, matrix products, shards(): lax.dot_general(dirb, kern, (((1,), (1,)), ((), ())), preferred_element_t...  15 us
    dot_general x1, matrix products, shards(): jnp.dot(fitted.astype(jnp.bfloat16), kern, preferred_element_type=jnp.flo...  12.8 us
  transfers between devices with their start and end apart: 4, of which 4 were waited for; matrix products, arithmetic and copies ran while one was open for 0% of the time, Pallas kernels for 0%

commit v1 on v0

v1 whole, which is shorter than its diff:
```python
import functools
import math

import jax
import jax.numpy as jnp
from jax import lax
from jax.experimental import pallas as pl
from jax.experimental.pallas import tpu as pltpu
from jax.sharding import PartitionSpec as P

MESH = pl.DeviceIdType.MESH
F32 = jnp.float32
BF16 = jnp.bfloat16
LOG2E = math.log2(math.e)

GROUPS = 4
PLANE = 16
DEPTH = 12
STRIDE = 3
PCH = 4
MCH = 4
LANES = 128


def three_terms(v):
    hi = v.astype(BF16)
    rest = v - hi.astype(F32)
    mid = rest.astype(BF16)
    lo = (rest - mid.astype(F32)).astype(BF16)
    return hi, mid, lo


def tail_rows(width, first, second):
    row = lax.broadcasted_iota(jnp.int32, (32, width), 0)
    out = jnp.zeros((32, width), F32)
    for k, v in enumerate((*first, *second)):
        out = jnp.where(row == k, v if isinstance(v, float) else v.astype(F32), out)
    return out.astype(BF16)


def kernel(
    pts_ref, cen_ref, dir_ref, res_ref, prec_ref, q_ref, scal_ref,
    xa, ca, dirb, kern, fits, col, rsb, z1b, z2b, agb, scb,
    fit_s, fit_r, rs_s, rs_r, z1_s, z1_r, z2_s, z2_r, ag_s, ag_r, sc_s, sc_r,
):
    npts = pts_ref.shape[1]
    ctrs = cen_ref.shape[1]
    tgt = dir_ref.shape[0]
    pch = npts // PCH
    mch = ctrs // MCH
    pts = lax.axis_index("pts")
    ctr = lax.axis_index("ctr")
    z = pts // PLANE
    mine = pts % PLANE
    third, step = z // STRIDE, z % STRIDE

    def ctr_peer(d):
        return {"ctr": (ctr + d) % GROUPS}

    def plane_peer(d):
        return {"pts": z * PLANE + (mine + d) % PLANE}

    def z_peer(d):
        return {"pts": (z + d) % DEPTH * PLANE + mine}

    barrier = pltpu.get_barrier_semaphore()
    peers = [ctr_peer(d) for d in range(1, GROUPS)]
    peers += [plane_peer(d) for d in range(1, PLANE)]
    peers += [z_peer(d) for d in (3, 6, 9, 1, 11)]
    for peer in peers:
        pl.semaphore_signal(barrier, inc=1, device_id=peer, device_id_type=MESH)

    def send(src, dst, s, r, peer):
        return pltpu.make_async_remote_copy(
            src_ref=src, dst_ref=dst, send_sem=s, recv_sem=r, device_id=peer, device_id_type=MESH
        )

    x32 = pts_ref[...].astype(F32)
    hi, mid, lo = three_terms(x32 * (0.25 * LOG2E))
    xa[0:32, :] = hi
    xa[32:64, :] = mid
    xa[64:96, :] = lo
    xsq = jnp.sum(x32 * x32, axis=0, keepdims=True) * (-0.125 * LOG2E)
    xa[96:128, :] = tail_rows(npts, (1.0, 1.0, 1.0), three_terms(xsq))

    def centre_block(k, carry):
        m0 = pl.multiple_of(k * 1024, 1024)
        c = cen_ref[:, pl.ds(m0, 1024)]
        c32 = c.astype(F32)
        csq = jnp.sum(c32 * c32, axis=0, keepdims=True) * (-0.125 * LOG2E)
        tail = tail_rows(1024, three_terms(csq), (1.0, 1.0, 1.0))
        ca[pl.ds(m0, 1024), :] = jnp.concatenate([c, c, c, tail], axis=0).T
        dirb[:, pl.ds(m0, 1024)] = dir_ref[:, pl.ds(m0, 1024)].astype(BF16)
        return carry

    lax.fori_loop(0, ctrs // 1024, centre_block, 0)

    def fit_copy(i, d):
        return send(
            fits.at[ctr, i], fits.at[ctr, i], fit_s.at[i, d], fit_r.at[i, d], ctr_peer(d)
        )

    def point_chunk(i):
        n0 = pl.multiple_of(i * pch, pch)

        def block(j, acc):
            m0 = pl.multiple_of(j * 2048, 2048)
            s = jnp.dot(
                ca[pl.ds(m0, 2048), :], xa[:, pl.ds(n0, pch)], preferred_element_type=F32
            )
            k = jnp.exp2(s).astype(BF16)
            kern[pl.ds(m0, 2048), pl.ds(n0, pch)] = k
            return acc + jnp.dot(dirb[:, pl.ds(m0, 2048)], k, preferred_element_type=F32)

        acc = lax.fori_loop(0, ctrs // 2048, block, jnp.zeros((tgt, pch), F32))
        fits[ctr, i] = acc.astype(BF16)

    def first_chunk(i, carry):
        point_chunk(i)
        for d in range(1, GROUPS):
            fit_copy(i, d).start()
        return carry

    point_chunk(0)
    pl.semaphore_wait(barrier, len(peers))
    for d in range(1, GROUPS):
        fit_copy(0, d).start()
    lax.fori_loop(1, PCH, first_chunk, 0)

    fitted = []
    for i in range(PCH):
        for d in range(1, GROUPS):
            fit_copy(i, d).wait()
        total = fits[0, i].astype(F32)
        for g in range(1, GROUPS):
            total = total + fits[g, i].astype(F32)
        fitted.append(total.astype(BF16))
    fitb = jnp.concatenate(fitted, axis=1)

    def rs_copy(c, d):
        return send(
            col.at[c, (mine + d) % PLANE], rsb.at[c, mine], rs_s.at[c, d], rs_r.at[c, d], plane_peer(d)
        )

    def ag_copy(c, d):
        return send(
            agb.at[c, mine], agb.at[c, mine], ag_s.at[c, d], ag_r.at[c, d], plane_peer(d)
        )

    def z1_copy(c, d):
        return send(
            z1b.at[c, third], z1b.at[c, third], z1_s.at[c, d], z1_r.at[c, d], z_peer(d * STRIDE)
        )

    def z2_copy(c, d):
        return send(
            z2b.at[c, step], z2b.at[c, step], z2_s.at[c, d], z2_r.at[c, d], z_peer((1, DEPTH - 1)[d])
        )

    def columns(c, carry):
        for h in range(mch // 512):
            m0 = pl.multiple_of(c * mch + h * 512, 512)
            part = lax.dot_general(
                fitb, kern[pl.ds(m0, 512), :], (((1,), (1,)), ((), ())), preferred_element_type=F32
            )
            for j in range(4):
                col[c, 4 * h + j] = part[:, j * LANES : (j + 1) * LANES]
        rsb[c, mine] = col[c, mine]
        for d in range(1, PLANE):
            rs_copy(c, d).start()
        return carry

    lax.fori_loop(0, MCH, columns, 0)

    def summed(ref, c, count):
        total = ref[c, 0]
        for k in range(1, count):
            total = total + ref[c, k]
        return total

    def to_z1(c, carry):
        for d in range(1, PLANE):
            rs_copy(c, d).wait()
        z1b[c, third] = summed(rsb, c, PLANE)
        for d in range(1, DEPTH // STRIDE):
            z1_copy(c, d).start()
        return carry

    def to_z2(c, carry):
        for d in range(1, DEPTH // STRIDE):
            z1_copy(c, d).wait()
        z2b[c, step] = summed(z1b, c, DEPTH // STRIDE)
        for d in range(2):
            z2_copy(c, d).start()
        return carry

    def to_ag(c, carry):
        for d in range(2):
            z2_copy(c, d).wait()
        agb[c, mine] = summed(z2b, c, STRIDE)
        for d in range(1, PLANE):
            ag_copy(c, d).start()
        return carry

    lax.fori_loop(0, MCH, to_z1, 0)
    lax.fori_loop(0, MCH, to_z2, 0)
    lax.fori_loop(0, MCH, to_ag, 0)

    scale = 2048.0 / (npts * DEPTH * PLANE)

    def finish(c, sums):
        for d in range(1, PLANE):
            ag_copy(c, d).wait()
        rr, rq, qq, dq = sums
        for k in range(PLANE):
            at = pl.ds(pl.multiple_of(c * mch + k * LANES, LANES), LANES)
            dirv, resv, prec = dir_ref[:, at], res_ref[:, at], prec_ref[:, at]
            image = agb[c, k] * scale + 0.5 * dirv
            q_ref[:, at] = image
            pr = prec * resv
            rr = rr + pr * resv
            rq = rq + pr * image
            qq = qq + prec * image * image
            dq = dq + dirv * image
        return rr, rq, qq, dq

    zero = jnp.zeros((tgt, LANES), F32)
    sums = lax.fori_loop(0, MCH, finish, (zero, zero, zero, zero))
    for k, v in enumerate(sums):
        scb[ctr, k] = v

    def sc_copy(d):
        return send(scb.at[ctr], scb.at[ctr], sc_s.at[d], sc_r.at[d], ctr_peer(d))

    for d in range(1, GROUPS):
        sc_copy(d).start()
    for d in range(1, GROUPS):
        sc_copy(d).wait()
    rr, rq, qq, dq = [
        jnp.sum(scb[0, k] + scb[1, k] + scb[2, k] + scb[3, k], axis=1, keepdims=True)
        for k in range(4)
    ]
    alpha = rr / dq
    rz_new = rr - 2.0 * alpha * rq + alpha * alpha * qq
    scal_ref[0] = jnp.broadcast_to(alpha, (tgt, LANES))
    scal_ref[1] = jnp.broadcast_to(rz_new / rr, (tgt, LANES))


def shards(points, centres, coef, resid, direction, precond):
    tgt, ctrs = direction.shape
    feat, npts = points.shape
    prec = precond[None, :]
    vm = pl.BlockSpec(memory_space=pltpu.VMEM)
    dma = pltpu.SemaphoreType.DMA
    share = (tgt, LANES)
    image, scal = pl.pallas_call(
        kernel,
        out_shape=(
            jax.ShapeDtypeStruct((tgt, ctrs), F32),
            jax.ShapeDtypeStruct((2, tgt, LANES), F32),
        ),
        in_specs=[vm] * 5,
        out_specs=(vm, vm),
        scratch_shapes=[
            pltpu.VMEM((128, npts), BF16),
            pltpu.VMEM((ctrs, 128), BF16),
            pltpu.VMEM((tgt, ctrs), BF16),
            pltpu.VMEM((ctrs, npts), BF16),
            pltpu.VMEM((GROUPS, PCH, tgt, npts // PCH), BF16),
            pltpu.VMEM((MCH, PLANE, *share), F32),
            pltpu.VMEM((MCH, PLANE, *share), F32),
            pltpu.VMEM((MCH, DEPTH // STRIDE, *share), F32),
            pltpu.VMEM((MCH, STRIDE, *share), F32),
            pltpu.VMEM((MCH, PLANE, *share), F32),
            pltpu.VMEM((GROUPS, 4, *share), F32),
            dma((PCH, GROUPS)), dma((PCH, GROUPS)),
            dma((MCH, PLANE)), dma((MCH, PLANE)),
            dma((MCH, DEPTH // STRIDE)), dma((MCH, DEPTH // STRIDE)),
            dma((MCH, 2)), dma((MCH, 2)),
            dma((MCH, PLANE)), dma((MCH, PLANE)),
            dma((GROUPS,)), dma((GROUPS,)),
        ],
        compiler_params=pltpu.CompilerParams(
            collective_id=0, has_side_effects=True, vmem_limit_bytes=60 << 20
        ),
        name="cg_step",
    )(points, centres, direction, resid, prec)
    alpha = scal[0, :, :1]
    beta = scal[1, :, :1]
    resid_new = resid - alpha * image
    return coef + alpha * direction, resid_new, prec * resid_new + beta * direction


def solution(mesh):
    return jax.shard_map(
        shards,
        mesh=mesh,
        in_specs=(P(None, "pts"), *[P(None, "ctr")] * 4, P("ctr")),
        out_specs=(P(None, "ctr"),) * 3,
        check_vma=False,
    )
```

time: 443 us -> 82.9 us (0.19)
  waiting for transfers between devices: 187 us -> 0 us
  blocking collectives: 150 us -> 0 us
  Pallas kernels: 0 us -> 78.7 us
  matrix products: 70.1 us -> 0 us
  local copies, waits for them, and re-layouts: 17 us -> 0.85 us
  between operations: 13.9 us -> 0.7 us
    reduce_scatter x3 -> x0, waiting for transfers between devices: 122 us -> none  [sum_in_order(): blocks = lax.psum_scatter(blocks, axes[k], scatter_dimension=0, tiled=True)]
    psum x10 -> x0, blocking collectives: 107 us -> none  [over_axes(): return functools.reduce(lax.psum, axes, x)]
    pallas_call x0 -> x1, Pallas kernels: none -> 78.7 us  [shards(): pl.pallas_call(kernel, out_shape=(jax.ShapeDtypeStruct((tgt, ctrs), F32),...]
    dot_general x10 -> x0, matrix products: 70.1 us -> none  [the longest x8 42.3 us: one_block(): lax.dot_general(block, centres, (((0,), (0,)), ((), ())), preferred_eleme...]
    all_gather x1 -> x0, waiting for transfers between devices: 65.4 us -> none  [gather_in_order(): blocks = lax.all_gather(blocks, axes[k])]
    all_gather x3 -> x0, blocking collectives: 42.6 us -> none  [the longest x2 25 us: gather_in_order(): blocks = lax.all_gather(blocks, axes[k])]
    transpose x3 -> x0, local copies, waits for them, and re-layouts: 8.54 us -> none  [the longest x1 3.55 us: joined_along(): blocks = jnp.moveaxis(blocks, 0, dim)]
    reshape x2 -> x0, local copies, waits for them, and re-layouts: 6.23 us -> none  [the longest x1 4.29 us: joined_along(): blocks.reshape(*shape[:dim], shape[dim] * shape[dim + 1], *shape[dim + 2:])]
  transfers between devices with their start and end apart: 4 -> 0, of which waited for: 4 -> 0; matrix products, arithmetic and copies ran while one was open for 0% -> 0% of each run, Pallas kernels for 0% -> 0%
where the time goes in v1:
time: 82.9 us; the launch traced here: 82.6 us
  Pallas kernels  78.7 us (95%)
  other arithmetic  2.35 us (3%)
  local copies, waits for them, and re-layouts  0.85 us (1%)
    pallas_call x1, Pallas kernels, shards(): pl.pallas_call(kernel, out_shape=(jax.ShapeDtypeStruct((tgt, ctrs), F32),...  78.7 us
    add x1, other arithmetic, shards(): prec * resid_new + beta * direction  2.35 us

profile of v1, /device:TPU:1, one launch (start us, length us, event | category | flops | bytes accessed | tf_op | source)
XLA Modules:
  0.0 82.6 jit_solution(4064641518963114753)
XLA Ops:
  0.6 0.0 copy-start
  0.6 0.0 copy-start.1
  0.7 0.0 copy-start.2
  0.7 0.0 copy-start.3
  0.7 78.7 %cg_step.1 = (f32[16,8192]{1,0:T(8,128)}, f32[2,16,128]{2,1,0:T(8,128)}) custom-call(bf16[32,2048]{1,0:T(8,128)(2,1)} %pts_ref.1, bf16[32,8192]{1,0:T(8,128)(2,1)} %cen_ref.1, f32[16,8192]{1,0:T(8,128)} %dir_ref.1, f32[16,8192]{1,0:T(8,128)} %res_ref.1, f32[1,8192]{1,0:T(1,128)} %bitcast.1), custom_call_target="tpu_custom_call" | custom-call | tf_op jit(solution)/shard_map/cg_step/pallas_call | solution.py:256
  79.4 0.8 %slice_reduce_fusion = (f32[16]{0:T(128)S(1)}, f32[16]{0:T(128)S(1)}) fusion(f32[2,16,128]{2,1,0:T(8,128)} %get-tuple-element.5), kind=kLoop, calls=%fused_computation.3 | loop fusion | bytes 256 | tf_op jit(solution)/shard_map/slice | solution.py:289
  80.2 0.0 copy-done
  80.2 0.0 copy-done.1
  80.3 0.0 copy-done.2
  80.3 0.0 copy-done.3
  80.3 2.3 %multiply_add_fusion = (f32[16,8192]{1,0:T(8,128)}, f32[16,8192]{1,0:T(8,128)}, f32[16,8192]{1,0:T(8,128)}) fusion(f32[16,8192]{1,0:T(8,128)S(1)} %copy-done, f32[16]{0:T(128)S(1)} %get-tuple-element.7, f32[8192]{0:T(1024)S(1)} %copy-done.3, f32[16,8192]{1,0:T(8,128)S(1)} %copy-done.1, f32[16,8192]{1,0:T(8,128)} %get-tuple-element.6, ...), kind=kLoop, calls=%fused_computation | loop fusion | flops 917504 | bytes 3702912 | tf_op jit(solution)/shard_map/add | solution.py:291
Async XLA Ops:
  0.6 79.6 %copy-start = (f32[16,8192]{1,0:T(8,128)S(1)}, f32[16,8192]{1,0:T(8,128)}, u32[]{:S(2)}) copy-start(f32[16,8192]{1,0:T(8,128)} %dir_ref.1) | copy-start | bytes 1572868
  0.6 79.6 %copy-start.1 = (f32[16,8192]{1,0:T(8,128)S(1)}, f32[16,8192]{1,0:T(8,128)}, u32[]{:S(2)}) copy-start(f32[16,8192]{1,0:T(8,128)} %res_ref.1) | copy-start | bytes 1572868
  0.7 79.6 %copy-start.2 = (f32[16,8192]{1,0:T(8,128)S(1)}, f32[16,8192]{1,0:T(8,128)}, u32[]{:S(2)}) copy-start(f32[16,8192]{1,0:T(8,128)} %param.8) | copy-start | bytes 1572868
  0.7 79.6 %copy-start.3 = (f32[8192]{0:T(1024)S(1)}, f32[8192]{0:T(1024)}, u32[]{:S(2)}) copy-start(f32[8192]{0:T(1024)} %param.11) | copy-start | bytes 98308

commit v2 on v1

v2 whole, which is shorter than its diff:
```python
import functools
import math

import jax
import jax.numpy as jnp
from jax import lax
from jax.experimental import pallas as pl
from jax.experimental.pallas import tpu as pltpu
from jax.sharding import PartitionSpec as P

MESH = pl.DeviceIdType.MESH
F32 = jnp.float32
BF16 = jnp.bfloat16
LOG2E = math.log2(math.e)

GROUPS = 4
PLANE = 16
DEPTH = 12
PCH = 4
MCH = 4
EARLY = 2
LANES = 128


def three_terms(v):
    hi = v.astype(BF16)
    rest = v - hi.astype(F32)
    mid = rest.astype(BF16)
    lo = (rest - mid.astype(F32)).astype(BF16)
    return hi, mid, lo


def tail_rows(width, first, second):
    row = lax.broadcasted_iota(jnp.int32, (32, width), 0)
    out = jnp.zeros((32, width), F32)
    for k, v in enumerate((*first, *second)):
        out = jnp.where(row == k, v if isinstance(v, float) else v.astype(F32), out)
    return out.astype(BF16)


def kernel(
    pts_hbm, cen_hbm, dir_hbm, res_hbm, prec_hbm, q_ref, scal_ref,
    pts_ref, cen_ref, dir_ref, res_ref, prec_ref,
    xa, ca, dirb, kern0, kern1, kern2, kern3, fits, early, col, rsb, zb, agb, scb,
    in_s, fit_s, fit_r, rs_s, rs_r, z_s, z_r, ag_s, ag_r, sc_s, sc_r,
):
    npts = pts_ref.shape[1]
    tgt, ctrs = dir_ref.shape
    pch = npts // PCH
    mch = ctrs // MCH
    kerns = (kern0, kern1, kern2, kern3)
    pts = lax.axis_index("pts")
    ctr = lax.axis_index("ctr")
    z = pts // PLANE
    mine = pts % PLANE

    loads = [
        pltpu.make_async_copy(src, dst, in_s.at[k])
        for k, (src, dst) in enumerate(
            [(pts_hbm, pts_ref), (cen_hbm, cen_ref), (dir_hbm, dir_ref), (res_hbm, res_ref), (prec_hbm, prec_ref)]
        )
    ]
    for load in loads:
        load.start()

    def ctr_peer(d):
        return {"ctr": (ctr + d) % GROUPS}

    def plane_peer(d):
        return {"pts": z * PLANE + (mine + d) % PLANE}

    def z_peer(d):
        return {"pts": (z + d) % DEPTH * PLANE + mine}

    barrier = pltpu.get_barrier_semaphore()
    peers = [ctr_peer(d) for d in range(1, GROUPS)]
    peers += [plane_peer(d) for d in range(1, PLANE)]
    peers += [z_peer(d) for d in range(1, DEPTH)]
    for peer in peers:
        pl.semaphore_signal(barrier, inc=1, device_id=peer, device_id_type=MESH)

    def send(src, dst, s, r, peer):
        return pltpu.make_async_remote_copy(
            src_ref=src, dst_ref=dst, send_sem=s, recv_sem=r, device_id=peer, device_id_type=MESH
        )

    loads[0].wait()
    x32 = pts_ref[...].astype(F32)
    hi, mid, lo = three_terms(x32 * (0.25 * LOG2E))
    xa[0:32, :] = hi
    xa[32:64, :] = mid
    xa[64:96, :] = lo
    xsq = jnp.sum(x32 * x32, axis=0, keepdims=True) * (-0.125 * LOG2E)
    xa[96:128, :] = tail_rows(npts, (1.0, 1.0, 1.0), three_terms(xsq))
    loads[1].wait()
    loads[2].wait()

    def centre_block(k, carry):
        m0 = pl.multiple_of(k * 1024, 1024)
        c = cen_ref[:, pl.ds(m0, 1024)]
        c32 = c.astype(F32)
        csq = jnp.sum(c32 * c32, axis=0, keepdims=True) * (-0.125 * LOG2E)
        tail = tail_rows(1024, three_terms(csq), (1.0, 1.0, 1.0))
        ca[pl.ds(m0, 1024), :] = jnp.concatenate([c, c, c, tail], axis=0).T
        dirb[:, pl.ds(m0, 1024)] = dir_ref[:, pl.ds(m0, 1024)].astype(BF16)
        return carry

    lax.fori_loop(0, ctrs // 1024, centre_block, 0)

    def fit_copy(i, d):
        return send(
            fits.at[ctr, i], fits.at[ctr, i], fit_s.at[i, d], fit_r.at[i, d], ctr_peer(d)
        )

    for i in range(PCH + 1):

        def block(j, acc, i=i):
            m0 = pl.multiple_of(j * 2048, 2048)
            if i < PCH:
                s = jnp.dot(
                    ca[pl.ds(m0, 2048), :], xa[:, i * pch : (i + 1) * pch], preferred_element_type=F32
                )
                kerns[i][pl.ds(m0, 2048), :] = jnp.exp2(s).astype(BF16)
            if i > 0:
                acc = acc + jnp.dot(
                    dirb[:, pl.ds(m0, 2048)], kerns[i - 1][pl.ds(m0, 2048), :], preferred_element_type=F32
                )
            return acc

        acc = lax.fori_loop(0, ctrs // 2048, block, jnp.zeros((tgt, pch), F32))
        if i == 1:
            pl.semaphore_wait(barrier, len(peers))
        if i > 0:
            fits[ctr, i - 1] = acc.astype(BF16)
            for d in range(1, GROUPS):
                fit_copy(i - 1, d).start()

    def fitted(i):
        for d in range(1, GROUPS):
            fit_copy(i, d).wait()
        total = fits[0, i].astype(F32)
        for g in range(1, GROUPS):
            total = total + fits[g, i].astype(F32)
        return total.astype(BF16)

    def rs_copy(c, d):
        return send(
            col.at[c, (mine + d) % PLANE], rsb.at[c, mine], rs_s.at[c, d], rs_r.at[c, d], plane_peer(d)
        )

    def z_copy(c, d):
        return send(zb.at[c, z], zb.at[c, z], z_s.at[c, d], z_r.at[c, d], z_peer(d))

    def ag_copy(c, d):
        return send(
            agb.at[c, mine], agb.at[c, mine], ag_s.at[c, d], ag_r.at[c, d], plane_peer(d)
        )

    def col_part(c, i, fit):
        return lax.dot_general(
            fit, kerns[i][c * mch : (c + 1) * mch, :], (((1,), (1,)), ((), ())), preferred_element_type=F32
        )

    def summed(ref, c, count):
        total = ref[c, 0]
        for k in range(1, count):
            total = total + ref[c, k]
        return total

    def to_rs(c, part):
        for j in range(PLANE):
            col[c, j] = part[:, j * LANES : (j + 1) * LANES]
        for d in range(1, PLANE):
            rs_copy(c, d).start()
        rsb[c, mine] = col[c, mine]

    def to_z(c):
        for d in range(1, PLANE):
            rs_copy(c, d).wait()
        zb[c, z] = summed(rsb, c, PLANE)
        for d in range(1, DEPTH):
            z_copy(c, d).start()

    def to_ag(c):
        for d in range(1, DEPTH):
            z_copy(c, d).wait()
        agb[c, mine] = summed(zb, c, DEPTH)
        for d in range(1, PLANE):
            ag_copy(c, d).start()

    fit = [fitted(i) for i in range(PCH - 1)]
    for c in range(EARLY):
        early[c] = sum((col_part(c, i, fit[i]) for i in range(1, PCH - 1)), col_part(c, 0, fit[0]))
    fit.append(fitted(PCH - 1))
    for c in range(EARLY):
        to_rs(c, early[c] + col_part(c, PCH - 1, fit[-1]))
    for c in range(EARLY, MCH):
        to_rs(c, sum((col_part(c, i, fit[i]) for i in range(1, PCH)), col_part(c, 0, fit[0])))
        if c == MCH - 2:
            to_z(0)
    to_z(1)
    to_z(2)
    to_ag(0)
    to_z(3)
    to_ag(1)
    to_ag(2)
    to_ag(3)

    scale = 2048.0 / (npts * DEPTH * PLANE)
    loads[3].wait()
    loads[4].wait()

    def finish(c, sums):
        for d in range(1, PLANE):
            ag_copy(c, d).wait()
        rr, rq, qq, dq = sums
        for k in range(PLANE):
            at = pl.ds(pl.multiple_of(c * mch + k * LANES, LANES), LANES)
            dirv, resv, prec = dir_ref[:, at], res_ref[:, at], prec_ref[:, at]
            image = agb[c, k] * scale + 0.5 * dirv
            q_ref[:, at] = image
            pr = prec * resv
            rr = rr + pr * resv
            rq = rq + pr * image
            qq = qq + prec * image * image
            dq = dq + dirv * image
        return rr, rq, qq, dq

    zero = jnp.zeros((tgt, LANES), F32)
    sums = lax.fori_loop(0, MCH, finish, (zero, zero, zero, zero))
    for k, v in enumerate(sums):
        scb[ctr, k] = v

    def sc_copy(d):
        return send(scb.at[ctr], scb.at[ctr], sc_s.at[d], sc_r.at[d], ctr_peer(d))

    for d in range(1, GROUPS):
        sc_copy(d).start()
    for d in range(1, GROUPS):
        sc_copy(d).wait()
    rr, rq, qq, dq = [
        jnp.sum(scb[0, k] + scb[1, k] + scb[2, k] + scb[3, k], axis=1, keepdims=True)
        for k in range(4)
    ]
    alpha = rr / dq
    rz_new = rr - 2.0 * alpha * rq + alpha * alpha * qq
    scal_ref[0] = jnp.broadcast_to(alpha, (tgt, LANES))
    scal_ref[1] = jnp.broadcast_to(rz_new / rr, (tgt, LANES))


def update(scal_ref, q_ref, coef_ref, res_ref, dir_ref, prec_ref, coef_out, res_out, dir_out):
    alpha, beta = scal_ref[0][:, :1], scal_ref[1][:, :1]
    dirv = dir_ref[...]
    res = res_ref[...] - alpha * q_ref[...]
    coef_out[...] = coef_ref[...] + alpha * dirv
    res_out[...] = res
    dir_out[...] = prec_ref[...] * res + beta * dirv


def shards(points, centres, coef, resid, direction, precond):
    tgt, ctrs = direction.shape
    npts = points.shape[1]
    prec = precond[None, :]
    vm = pl.BlockSpec(memory_space=pltpu.VMEM)
    dma = pltpu.SemaphoreType.DMA
    share = (tgt, LANES)
    whole = jax.ShapeDtypeStruct((tgt, ctrs), F32)
    args = (points, centres, direction, resid, prec)
    image, scal = pl.pallas_call(
        kernel,
        out_shape=(whole, jax.ShapeDtypeStruct((2, *share), F32)),
        in_specs=[pl.BlockSpec(memory_space=pl.ANY)] * 5,
        out_specs=(vm, vm),
        scratch_shapes=[
            *[pltpu.VMEM(a.shape, a.dtype) for a in args],
            pltpu.VMEM((128, npts), BF16),
            pltpu.VMEM((ctrs, 128), BF16),
            pltpu.VMEM((tgt, ctrs), BF16),
            *[pltpu.VMEM((ctrs, npts // PCH), BF16)] * PCH,
            pltpu.VMEM((GROUPS, PCH, tgt, npts // PCH), BF16),
            pltpu.VMEM((EARLY, tgt, ctrs // MCH), F32),
            pltpu.VMEM((MCH, PLANE, *share), F32),
            pltpu.VMEM((MCH, PLANE, *share), F32),
            pltpu.VMEM((MCH, DEPTH, *share), F32),
            pltpu.VMEM((MCH, PLANE, *share), F32),
            pltpu.VMEM((GROUPS, 4, *share), F32),
            dma((5,)),
            dma((PCH, GROUPS)), dma((PCH, GROUPS)),
            dma((MCH, PLANE)), dma((MCH, PLANE)),
            dma((MCH, DEPTH)), dma((MCH, DEPTH)),
            dma((MCH, PLANE)), dma((MCH, PLANE)),
            dma((GROUPS,)), dma((GROUPS,)),
        ],
        compiler_params=pltpu.CompilerParams(
            collective_id=0, has_side_effects=True, vmem_limit_bytes=48 << 20
        ),
        name="cg_step",
    )(*args)
    return pl.pallas_call(
        update,
        out_shape=(whole,) * 3,
        in_specs=[vm] * 6,
        out_specs=(vm,) * 3,
        compiler_params=pltpu.CompilerParams(vmem_limit_bytes=8 << 20),
        name="update",
    )(scal, image, coef, resid, direction, prec)


def solution(mesh):
    return jax.shard_map(
        shards,
        mesh=mesh,
        in_specs=(P(None, "pts"), *[P(None, "ctr")] * 4, P("ctr")),
        out_specs=(P(None, "ctr"),) * 3,
        check_vma=False,
    )
```

time: 82.9 us -> 82.1 us (level)
  local copies, waits for them, and re-layouts: 0.85 us -> 4.78 us
  Pallas kernels: 78.7 us -> 76.3 us
  other arithmetic: 2.35 us -> 0 us
    unnamed x8 -> x12, local copies, waits for them, and re-layouts: 0.02 us -> 4.78 us
    pallas_call x1 -> x2, Pallas kernels: 78.7 us -> 76.3 us  [the longest x1 75 us: shards(): pl.pallas_call(kernel, out_shape=(whole, jax.ShapeDtypeStruct((2, *share)...]
    add x1 -> x0, other arithmetic: 2.35 us -> none  [shards(): prec * resid_new + beta * direction]
where the time goes in v2:
time: 82.1 us; the launch traced here: 81.7 us
  Pallas kernels  76.3 us (93%)
  local copies, waits for them, and re-layouts  4.78 us (6%)
    pallas_call x1, Pallas kernels, shards(): pl.pallas_call(kernel, out_shape=(whole, jax.ShapeDtypeStruct((2, *share)...  75 us
    unnamed x12, local copies, waits for them, and re-layouts  4.78 us

profile of v2, /device:TPU:1, one launch (start us, length us, event | category | flops | bytes accessed | tf_op | source)
XLA Modules:
  0.0 81.7 jit_solution(17734754133498633672)
XLA Ops:
  0.6 0.0 copy-start
  0.6 1.0 %copy-done = f32[16,8192]{1,0:T(8,128)S(1)} copy-done((f32[16,8192]{1,0:T(8,128)S(1)}, f32[16,8192]{1,0:T(8,128)}, u32[]{:S(2)}) %copy-start) | copy-done | bytes 524312
  1.7 0.0 copy-start.1
  1.7 1.0 %copy-done.1 = f32[16,8192]{1,0:T(8,128)S(1)} copy-done((f32[16,8192]{1,0:T(8,128)S(1)}, f32[16,8192]{1,0:T(8,128)}, u32[]{:S(2)}) %copy-start.1) | copy-done | bytes 524312
  2.7 0.0 copy-start.2
  2.7 1.0 %copy-done.2 = bf16[32,8192]{1,0:T(8,128)(2,1)S(1)} copy-done((bf16[32,8192]{1,0:T(8,128)(2,1)S(1)}, bf16[32,8192]{1,0:T(8,128)(2,1)}, u32[]{:S(2)}) %copy-start.2) | copy-done | bytes 524312
  3.8 0.0 copy-start.4
  3.8 0.8 copy-done.4
  4.5 0.0 copy-start.5
  4.5 0.9 %copy-done.5 = bf16[32,2048]{1,0:T(8,128)(2,1)S(1)} copy-done((bf16[32,2048]{1,0:T(8,128)(2,1)S(1)}, bf16[32,2048]{1,0:T(8,128)(2,1)}, u32[]{:S(2)}) %copy-start.5) | copy-done | bytes 131096
  5.4 0.0 copy-start.3
  5.4 75.0 %cg_step.1 = (f32[16,8192]{1,0:T(8,128)S(1)}, f32[2,16,128]{2,1,0:T(8,128)S(1)}) custom-call(bf16[32,2048]{1,0:T(8,128)(2,1)S(1)} %copy-done.5, bf16[32,8192]{1,0:T(8,128)(2,1)S(1)} %copy-done.2, f32[16,8192]{1,0:T(8,128)S(1)} %copy-done, f32[16,8192]{1,0:T(8,128)S(1)} %copy-done.1, f32[1,8192]{1,0:T(1,128)S(1)} %bitcast.1), custom_call_target="tpu_custom_call" | custom-call | tf_op jit(solution)/shard_map/cg_step/pallas_call | solution.py:269
  80.4 0.0 copy-done.3
  80.4 1.3 %update.1 = (f32[16,8192]{1,0:T(8,128)}, f32[16,8192]{1,0:T(8,128)}, f32[16,8192]{1,0:T(8,128)}) custom-call(f32[2,16,128]{2,1,0:T(8,128)S(1)} %get-tuple-element.5.scal_ref, f32[16,8192]{1,0:T(8,128)S(1)} %get-tuple-element.6.q_ref, f32[16,8192]{1,0:T(8,128)S(1)} %copy-done.3, f32[16,8192]{1,0:T(8,128)S(1)} %copy-done.1, f32[16,8192]{1,0:T(8,128)S(1)} %copy-done, ...), custom_call_target="tpu_custom_call" | custom-call | tf_op jit(solution)/shard_map/update/pallas_call | solution.py:299
Async XLA Ops:
  0.6 1.0 %copy-start = (f32[16,8192]{1,0:T(8,128)S(1)}, f32[16,8192]{1,0:T(8,128)}, u32[]{:S(2)}) copy-start(f32[16,8192]{1,0:T(8,128)} %dir_ref.1) | copy-start | bytes 1572868
  1.7 1.0 %copy-start.1 = (f32[16,8192]{1,0:T(8,128)S(1)}, f32[16,8192]{1,0:T(8,128)}, u32[]{:S(2)}) copy-start(f32[16,8192]{1,0:T(8,128)} %res_ref.1) | copy-start | bytes 1572868
  2.7 1.0 %copy-start.2 = (bf16[32,8192]{1,0:T(8,128)(2,1)S(1)}, bf16[32,8192]{1,0:T(8,128)(2,1)}, u32[]{:S(2)}) copy-start(bf16[32,8192]{1,0:T(8,128)(2,1)} %cen_hbm.1) | copy-start | bytes 1572868
  3.8 0.8 copy-start.4
  4.5 0.9 %copy-start.5 = (bf16[32,2048]{1,0:T(8,128)(2,1)S(1)}, bf16[32,2048]{1,0:T(8,128)(2,1)}, u32[]{:S(2)}) copy-start(bf16[32,2048]{1,0:T(8,128)(2,1)} %pts_hbm.1) | copy-start | bytes 393220
  5.4 75.0 %copy-start.3 = (f32[16,8192]{1,0:T(8,128)S(1)}, f32[16,8192]{1,0:T(8,128)}, u32[]{:S(2)}) copy-start(f32[16,8192]{1,0:T(8,128)} %coef_ref.1) | copy-start | bytes 1572868

commit v3 on v2

--- a/solution.py
+++ b/solution.py
@@ -16,9 +16,11 @@
 GROUPS = 4
 PLANE = 16
 DEPTH = 12
+STRIDE = 3
 PCH = 4
 MCH = 4
 EARLY = 2
+UCH = 2
 LANES = 128
 
 
@@ -39,10 +41,10 @@
 
 
 def kernel(
-    pts_hbm, cen_hbm, dir_hbm, res_hbm, prec_hbm, q_ref, scal_ref,
-    pts_ref, cen_ref, dir_ref, res_ref, prec_ref,
-    xa, ca, dirb, kern0, kern1, kern2, kern3, fits, early, col, rsb, zb, agb, scb,
-    in_s, fit_s, fit_r, rs_s, rs_r, z_s, z_r, ag_s, ag_r, sc_s, sc_r,
+    pts_hbm, cen_hbm, dir_hbm, res_hbm, prec_hbm, q_hbm, scal_ref,
+    pts_ref, cen_ref, dir_ref, res_ref, prec_ref, q_ref,
+    xa, ca, dirb, kern0, kern1, kern2, kern3, fits, early, col, rsb, z1b, z2b, agb, scb, spb,
+    in_s, out_s, fit_s, fit_r, rs_s, rs_r, z1_s, z1_r, z2_s, z2_r, ag_s, ag_r, sc_s, sc_r, sp_s, sp_r,
 ):
     npts = pts_ref.shape[1]
     tgt, ctrs = dir_ref.shape
@@ -53,6 +55,7 @@
     ctr = lax.axis_index("ctr")
     z = pts // PLANE
     mine = pts % PLANE
+    third, step = z // STRIDE, z % STRIDE
 
     loads = [
         pltpu.make_async_copy(src, dst, in_s.at[k])
@@ -75,7 +78,7 @@
     barrier = pltpu.get_barrier_semaphore()
     peers = [ctr_peer(d) for d in range(1, GROUPS)]
     peers += [plane_peer(d) for d in range(1, PLANE)]
-    peers += [z_peer(d) for d in range(1, DEPTH)]
+    peers += [z_peer(d) for d in (3, 6, 9, 1, 11)]
     for peer in peers:
         pl.semaphore_signal(barrier, inc=1, device_id=peer, device_id_type=MESH)
 
@@ -113,25 +116,15 @@
         )
 
     for i in range(PCH + 1):
-
-        def block(j, acc, i=i):
-            m0 = pl.multiple_of(j * 2048, 2048)
-            if i < PCH:
-                s = jnp.dot(
-                    ca[pl.ds(m0, 2048), :], xa[:, i * pch : (i + 1) * pch], preferred_element_type=F32
-                )
-                kerns[i][pl.ds(m0, 2048), :] = jnp.exp2(s).astype(BF16)
-            if i > 0:
-                acc = acc + jnp.dot(
-                    dirb[:, pl.ds(m0, 2048)], kerns[i - 1][pl.ds(m0, 2048), :], preferred_element_type=F32
-                )
-            return acc
-
-        acc = lax.fori_loop(0, ctrs // 2048, block, jnp.zeros((tgt, pch), F32))
+        if i < PCH:
+            s = jnp.dot(ca[...], xa[:, i * pch : (i + 1) * pch], preferred_element_type=F32)
+            kerns[i][...] = jnp.exp2(s).astype(BF16)
+        if i > 0:
+            part = jnp.dot(dirb[...], kerns[i - 1][...], preferred_element_type=F32)
         if i == 1:
             pl.semaphore_wait(barrier, len(peers))
         if i > 0:
-            fits[ctr, i - 1] = acc.astype(BF16)
+            fits[ctr, i - 1] = part.astype(BF16)
             for d in range(1, GROUPS):
                 fit_copy(i - 1, d).start()
 
@@ -148,8 +141,15 @@
             col.at[c, (mine + d) % PLANE], rsb.at[c, mine], rs_s.at[c, d], rs_r.at[c, d], plane_peer(d)
         )
 
-    def z_copy(c, d):
-        return send(zb.at[c, z], zb.at[c, z], z_s.at[c, d], z_r.at[c, d], z_peer(d))
+    def z1_copy(c, d):
+        return send(
+            z1b.at[c, third], z1b.at[c, third], z1_s.at[c, d], z1_r.at[c, d], z_peer(d * STRIDE)
+        )
+
+    def z2_copy(c, d):
+        return send(
+            z2b.at[c, step], z2b.at[c, step], z2_s.at[c, d], z2_r.at[c, d], z_peer((1, DEPTH - 1)[d])
+        )
 
     def ag_copy(c, d):
         return send(
@@ -174,19 +174,35 @@
             rs_copy(c, d).start()
         rsb[c, mine] = col[c, mine]
 
-    def to_z(c):
+    def to_z1(c):
         for d in range(1, PLANE):
             rs_copy(c, d).wait()
-        zb[c, z] = summed(rsb, c, PLANE)
-        for d in range(1, DEPTH):
-            z_copy(c, d).start()
-
-    def to_ag(c):
-        for d in range(1, DEPTH):
-            z_copy(c, d).wait()
-        agb[c, mine] = summed(zb, c, DEPTH)
+        z1b[c, third] = summed(rsb, c, PLANE)
+        for d in range(1, DEPTH // STRIDE):
+            z1_copy(c, d).start()
+
+    def to_z2(c):
+        for d in range(1, DEPTH // STRIDE):
+            z1_copy(c, d).wait()
+        z2b[c, step] = summed(z1b, c, DEPTH // STRIDE)
+        for d in range(2):
+            z2_copy(c, d).start()
+
+    scale = 2048.0 / (npts * DEPTH * PLANE)
+
+    def to_ag(c, sums):
+        for d in range(2):
+            z2_copy(c, d).wait()
+        share = summed(z2b, c, STRIDE)
+        agb[c, mine] = share
         for d in range(1, PLANE):
             ag_copy(c, d).start()
+        at = pl.ds(pl.multiple_of(c * mch + mine * LANES, LANES), LANES)
+        dirv, resv, prec = dir_ref[:, at], res_ref[:, at], prec_ref[:, at]
+        image = share * scale + 0.5 * dirv
+        pr = prec * resv
+        new = (pr * resv, pr * image, prec * image * image, dirv * image)
+        return [a + b for a, b in zip(sums, new)]
 
     fit = [fitted(i) for i in range(PCH - 1)]
     for c in range(EARLY):
@@ -197,55 +213,70 @@
     for c in range(EARLY, MCH):
         to_rs(c, sum((col_part(c, i, fit[i]) for i in range(1, PCH)), col_part(c, 0, fit[0])))
         if c == MCH - 2:
-            to_z(0)
-    to_z(1)
-    to_z(2)
-    to_ag(0)
-    to_z(3)
-    to_ag(1)
-    to_ag(2)
-    to_ag(3)
-
-    scale = 2048.0 / (npts * DEPTH * PLANE)
+            to_z1(0)
     loads[3].wait()
     loads[4].wait()
-
-    def finish(c, sums):
-        for d in range(1, PLANE):
-            ag_copy(c, d).wait()
-        rr, rq, qq, dq = sums
-        for k in range(PLANE):
-            at = pl.ds(pl.multiple_of(c * mch + k * LANES, LANES), LANES)
-            dirv, resv, prec = dir_ref[:, at], res_ref[:, at], prec_ref[:, at]
-            image = agb[c, k] * scale + 0.5 * dirv
-            q_ref[:, at] = image
-            pr = prec * resv
-            rr = rr + pr * resv
-            rq = rq + pr * image
-            qq = qq + prec * image * image
-            dq = dq + dirv * image
-        return rr, rq, qq, dq
-
-    zero = jnp.zeros((tgt, LANES), F32)
-    sums = lax.fori_loop(0, MCH, finish, (zero, zero, zero, zero))
+    sums = [jnp.zeros((tgt, LANES), F32)] * 4
+    to_z1(1)
+    to_z2(0)
+    to_z1(2)
+    to_z2(1)
+    sums = to_ag(0, sums)
+    to_z1(3)
+    to_z2(2)
+    sums = to_ag(1, sums)
+    to_z2(3)
+    sums = to_ag(2, sums)
+    sums = to_ag(3, sums)
+
+    lane = lax.broadcasted_iota(jnp.int32, (tgt, LANES), 1)
+    packed = jnp.zeros((tgt, LANES), F32)
     for k, v in enumerate(sums):
-        scb[ctr, k] = v
+        packed = jnp.where(lane == k, jnp.sum(v, axis=1, keepdims=True), packed)
+    scb[ctr] = packed
 
     def sc_copy(d):
         return send(scb.at[ctr], scb.at[ctr], sc_s.at[d], sc_r.at[d], ctr_peer(d))
+
+    def sp_copy(d):
+        return send(spb.at[mine], spb.at[mine], sp_s.at[d], sp_r.at[d], plane_peer(d))
 
     for d in range(1, GROUPS):
         sc_copy(d).start()
     for d in range(1, GROUPS):
         sc_copy(d).wait()
+    spb[mine] = scb[0] + scb[1] + scb[2] + scb[3]
+    for d in range(1, PLANE):
+        sp_copy(d).start()
+
+    def out_copy(c):
+        at = pl.ds(pl.multiple_of(c * mch, mch), mch)
+        return pltpu.make_async_copy(q_ref.at[:, at], q_hbm.at[:, at], out_s.at[c])
+
+    def finish(c, carry):
+        for d in range(1, PLANE):
+            ag_copy(c, d).wait()
+        for k in range(PLANE):
+            at = pl.ds(pl.multiple_of(c * mch + k * LANES, LANES), LANES)
+            q_ref[:, at] = agb[c, k] * scale + 0.5 * dir_ref[:, at]
+        out_copy(c).start()
+        return carry
+
+    lax.fori_loop(0, MCH, finish, 0)
+    for d in range(1, PLANE):
+        sp_copy(d).wait()
+    packed = spb[0]
+    for k in range(1, PLANE):
+        packed = packed + spb[k]
     rr, rq, qq, dq = [
-        jnp.sum(scb[0, k] + scb[1, k] + scb[2, k] + scb[3, k], axis=1, keepdims=True)
-        for k in range(4)
+        jnp.sum(jnp.where(lane == k, packed, 0.0), axis=1, keepdims=True) for k in range(4)
     ]
     alpha = rr / dq
     rz_new = rr - 2.0 * alpha * rq + alpha * alpha * qq
     scal_ref[0] = jnp.broadcast_to(alpha, (tgt, LANES))
     scal_ref[1] = jnp.broadcast_to(rz_new / rr, (tgt, LANES))
+    for c in range(MCH):
+        out_copy(c).wait()
 
 
 def update(scal_ref, q_ref, coef_ref, res_ref, dir_ref, prec_ref, coef_out, res_out, dir_out):
@@ -270,9 +301,10 @@
         kernel,
         out_shape=(whole, jax.ShapeDtypeStruct((2, *share), F32)),
         in_specs=[pl.BlockSpec(memory_space=pl.ANY)] * 5,
-        out_specs=(vm, vm),
+        out_specs=(pl.BlockSpec(memory_space=pl.ANY), vm),
         scratch_shapes=[
             *[pltpu.VMEM(a.shape, a.dtype) for a in args],
+            pltpu.VMEM((tgt, ctrs), F32),
             pltpu.VMEM((128, npts), BF16),
             pltpu.VMEM((ctrs, 128), BF16),
             pltpu.VMEM((tgt, ctrs), BF16),
@@ -281,27 +313,37 @@
             pltpu.VMEM((EARLY, tgt, ctrs // MCH), F32),
             pltpu.VMEM((MCH, PLANE, *share), F32),
             pltpu.VMEM((MCH, PLANE, *share), F32),
-            pltpu.VMEM((MCH, DEPTH, *share), F32),
+            pltpu.VMEM((MCH, DEPTH // STRIDE, *share), F32),
+            pltpu.VMEM((MCH, STRIDE, *share), F32),
             pltpu.VMEM((MCH, PLANE, *share), F32),
-            pltpu.VMEM((GROUPS, 4, *share), F32),
+            pltpu.VMEM((GROUPS, *share), F32),
+            pltpu.VMEM((PLANE, *share), F32),
             dma((5,)),
+            dma((MCH,)),
             dma((PCH, GROUPS)), dma((PCH, GROUPS)),
             dma((MCH, PLANE)), dma((MCH, PLANE)),
-            dma((MCH, DEPTH)), dma((MCH, DEPTH)),
+            dma((MCH, DEPTH // STRIDE)), dma((MCH, DEPTH // STRIDE)),
+            dma((MCH, 2)), dma((MCH, 2)),
             dma((MCH, PLANE)), dma((MCH, PLANE)),
             dma((GROUPS,)), dma((GROUPS,)),
+            dma((PLANE,)), dma((PLANE,)),
         ],
         compiler_params=pltpu.CompilerParams(
-            collective_id=0, has_side_effects=True, vmem_limit_bytes=48 << 20
+            collective_id=0, has_side_effects=True, vmem_limit_bytes=56 << 20
         ),
         name="cg_step",
     )(*args)
     return pl.pallas_call(
         update,
         out_shape=(whole,) * 3,
-        in_specs=[vm] * 6,
-        out_specs=(vm,) * 3,
-        compiler_params=pltpu.CompilerParams(vmem_limit_bytes=8 << 20),
+        grid=(UCH,),
+        in_specs=[
+            pl.BlockSpec((2, *share), lambda k: (0, 0, 0)),
+            *[pl.BlockSpec((tgt, ctrs // UCH), lambda k: (0, k))] * 4,
+            pl.BlockSpec((1, ctrs // UCH), lambda k: (0, k)),
+        ],
+        out_specs=(pl.BlockSpec((tgt, ctrs // UCH), lambda k: (0, k)),) * 3,
+        compiler_params=pltpu.CompilerParams(vmem_limit_bytes=60 << 20),
         name="update",
     )(scal, image, coef, resid, direction, prec)
 

time: 82.1 us -> 81.7 us (level)
  local copies, waits for them, and re-layouts: 4.78 us -> 0 us
  Pallas kernels: 76.3 us -> 80.9 us
    unnamed x12 -> x0, local copies, waits for them, and re-layouts: 4.78 us -> none
    pallas_call x1, Pallas kernels: 75 us -> 78.3 us  [shards(): pl.pallas_call(kernel, out_shape=(whole, jax.ShapeDtypeStruct((2, *share)...]
    pallas_call x1, Pallas kernels: 1.31 us -> 2.57 us  [shards(): pl.pallas_call(update, out_shape=(whole,) * 3, grid=(UCH,), in_specs=[pl....]
where the time goes in v3:
time: 81.7 us; the launch traced here: 81.5 us
  Pallas kernels  80.9 us (99%)
    pallas_call x1, Pallas kernels, shards(): pl.pallas_call(kernel, out_shape=(whole, jax.ShapeDtypeStruct((2, *share)...  78.3 us
    pallas_call x1, Pallas kernels, shards(): pl.pallas_call(update, out_shape=(whole,) * 3, grid=(UCH,), in_specs=[pl....  2.57 us

profile of v3, /device:TPU:1, one launch (start us, length us, event | category | flops | bytes accessed | tf_op | source)
XLA Modules:
  0.0 81.5 jit_solution(12997271450958295919)
XLA Ops:
  0.6 78.3 %cg_step.1 = (f32[16,8192]{1,0:T(8,128)}, f32[2,16,128]{2,1,0:T(8,128)}) custom-call(bf16[32,2048]{1,0:T(8,128)(2,1)} %pts_hbm.1, bf16[32,8192]{1,0:T(8,128)(2,1)} %cen_hbm.1, f32[16,8192]{1,0:T(8,128)} %dir_ref.1, f32[16,8192]{1,0:T(8,128)} %res_ref.1, f32[1,8192]{1,0:T(1,128)} %bitcast.1), custom_call_target="tpu_custom_call" | custom-call | tf_op jit(solution)/shard_map/cg_step/pallas_call | solution.py:300
  78.9 2.6 %update.1 = (f32[16,8192]{1,0:T(8,128)}, f32[16,8192]{1,0:T(8,128)}, f32[16,8192]{1,0:T(8,128)}) custom-call(f32[2,16,128]{2,1,0:T(8,128)} %get-tuple-element.5.scal_ref, f32[16,8192]{1,0:T(8,128)} %get-tuple-element.6.q_ref, f32[16,8192]{1,0:T(8,128)} %coef_ref.1, f32[16,8192]{1,0:T(8,128)} %res_ref.1, f32[16,8192]{1,0:T(8,128)} %dir_ref.1, f32[1,8192]{1,0:T(1,128)} %bitcast.2), custom_call_target="tpu_custom_call" | custom-call | tf_op jit(solution)/shard_map/update/pallas_call | solution.py:336

commit v4 on v3

--- a/solution.py
+++ b/solution.py
@@ -190,13 +190,17 @@
 
     scale = 2048.0 / (npts * DEPTH * PLANE)
 
+    def start_ag(c):
+        for d in range(1, PLANE):
+            ag_copy(c, d).start()
+
     def to_ag(c, sums):
         for d in range(2):
             z2_copy(c, d).wait()
         share = summed(z2b, c, STRIDE)
         agb[c, mine] = share
-        for d in range(1, PLANE):
-            ag_copy(c, d).start()
+        if c < MCH - 1:
+            start_ag(c)
         at = pl.ds(pl.multiple_of(c * mch + mine * LANES, LANES), LANES)
         dirv, resv, prec = dir_ref[:, at], res_ref[:, at], prec_ref[:, at]
         image = share * scale + 0.5 * dirv
@@ -230,24 +234,29 @@
     sums = to_ag(3, sums)
 
     lane = lax.broadcasted_iota(jnp.int32, (tgt, LANES), 1)
+    spot = lane - lax.broadcasted_iota(jnp.int32, (tgt, LANES), 0)
     packed = jnp.zeros((tgt, LANES), F32)
     for k, v in enumerate(sums):
-        packed = jnp.where(lane == k, jnp.sum(v, axis=1, keepdims=True), packed)
-    scb[ctr] = packed
+        packed = jnp.where(spot == k * tgt, jnp.sum(v, axis=1, keepdims=True), packed)
+    spb[mine] = jnp.sum(packed, axis=0, keepdims=True)
+
+    def sp_copy(d):
+        return send(spb.at[mine], spb.at[mine], sp_s.at[d], sp_r.at[d], plane_peer(d))
 
     def sc_copy(d):
         return send(scb.at[ctr], scb.at[ctr], sc_s.at[d], sc_r.at[d], ctr_peer(d))
 
-    def sp_copy(d):
-        return send(spb.at[mine], spb.at[mine], sp_s.at[d], sp_r.at[d], plane_peer(d))
-
+    for d in range(1, PLANE):
+        sp_copy(d).start()
+    start_ag(MCH - 1)
+    for d in range(1, PLANE):
+        sp_copy(d).wait()
+    total = spb[0]
+    for k in range(1, PLANE):
+        total = total + spb[k]
+    scb[ctr] = total
     for d in range(1, GROUPS):
         sc_copy(d).start()
-    for d in range(1, GROUPS):
-        sc_copy(d).wait()
-    spb[mine] = scb[0] + scb[1] + scb[2] + scb[3]
-    for d in range(1, PLANE):
-        sp_copy(d).start()
 
     def out_copy(c):
         at = pl.ds(pl.multiple_of(c * mch, mch), mch)
@@ -263,13 +272,11 @@
         return carry
 
     lax.fori_loop(0, MCH, finish, 0)
-    for d in range(1, PLANE):
-        sp_copy(d).wait()
-    packed = spb[0]
-    for k in range(1, PLANE):
-        packed = packed + spb[k]
+    for d in range(1, GROUPS):
+        sc_copy(d).wait()
+    total = scb[0] + scb[1] + scb[2] + scb[3]
     rr, rq, qq, dq = [
-        jnp.sum(jnp.where(lane == k, packed, 0.0), axis=1, keepdims=True) for k in range(4)
+        jnp.sum(jnp.where(spot == k * tgt, total, 0.0), axis=1, keepdims=True) for k in range(4)
     ]
     alpha = rr / dq
     rz_new = rr - 2.0 * alpha * rq + alpha * alpha * qq
@@ -316,8 +323,8 @@
             pltpu.VMEM((MCH, DEPTH // STRIDE, *share), F32),
             pltpu.VMEM((MCH, STRIDE, *share), F32),
             pltpu.VMEM((MCH, PLANE, *share), F32),
-            pltpu.VMEM((GROUPS, *share), F32),
-            pltpu.VMEM((PLANE, *share), F32),
+            pltpu.VMEM((GROUPS, 1, LANES), F32),
+            pltpu.VMEM((PLANE, 1, LANES), F32),
             dma((5,)),
             dma((MCH,)),
             dma((PCH, GROUPS)), dma((PCH, GROUPS)),

time: 81.7 us -> 80.1 us (0.980)
  Pallas kernels: 80.9 us -> 79.3 us
    pallas_call x1, Pallas kernels: 78.3 us -> 76.7 us  [shards(): pl.pallas_call(kernel, out_shape=(whole, jax.ShapeDtypeStruct((2, *share)...]
where the time goes in v4:
time: 80.1 us; the launch traced here: 79.9 us
  Pallas kernels  79.3 us (99%)
    pallas_call x1, Pallas kernels, shards(): pl.pallas_call(kernel, out_shape=(whole, jax.ShapeDtypeStruct((2, *share)...  76.7 us
    pallas_call x1, Pallas kernels, shards(): pl.pallas_call(update, out_shape=(whole,) * 3, grid=(UCH,), in_specs=[pl....  2.57 us

profile of v4, /device:TPU:1, one launch (start us, length us, event | category | flops | bytes accessed | tf_op | source)
XLA Modules:
  0.0 79.9 jit_solution(8586327987417970001)
XLA Ops:
  0.6 76.7 %cg_step.1 = (f32[16,8192]{1,0:T(8,128)}, f32[2,16,128]{2,1,0:T(8,128)}) custom-call(bf16[32,2048]{1,0:T(8,128)(2,1)} %pts_hbm.1, bf16[32,8192]{1,0:T(8,128)(2,1)} %cen_hbm.1, f32[16,8192]{1,0:T(8,128)} %dir_ref.1, f32[16,8192]{1,0:T(8,128)} %res_ref.1, f32[1,8192]{1,0:T(1,128)} %bitcast.1), custom_call_target="tpu_custom_call" | custom-call | tf_op jit(solution)/shard_map/cg_step/pallas_call | solution.py:307
  77.4 2.6 %update.1 = (f32[16,8192]{1,0:T(8,128)}, f32[16,8192]{1,0:T(8,128)}, f32[16,8192]{1,0:T(8,128)}) custom-call(f32[2,16,128]{2,1,0:T(8,128)} %get-tuple-element.5.scal_ref, f32[16,8192]{1,0:T(8,128)} %get-tuple-element.6.q_ref, f32[16,8192]{1,0:T(8,128)} %coef_ref.1, f32[16,8192]{1,0:T(8,128)} %res_ref.1, f32[16,8192]{1,0:T(8,128)} %dir_ref.1, f32[1,8192]{1,0:T(1,128)} %bitcast.2), custom_call_target="tpu_custom_call" | custom-call | tf_op jit(solution)/shard_map/update/pallas_call | solution.py:343

commit v5 on v4

--- a/solution.py
+++ b/solution.py
@@ -22,6 +22,9 @@
 EARLY = 2
 UCH = 2
 LANES = 128
+CROWS = 2048
+IN_PLANE = (4, 12, 3, 5, 11, 13, 2, 6, 10, 14, 1, 7, 9, 15, 8)
+ALONG_Z = (6, 5, 7, 4, 8, 3, 9, 2, 10, 1, 11)
 
 
 def three_terms(v):
@@ -43,8 +46,8 @@
 def kernel(
     pts_hbm, cen_hbm, dir_hbm, res_hbm, prec_hbm, q_hbm, scal_ref,
     pts_ref, cen_ref, dir_ref, res_ref, prec_ref, q_ref,
-    xa, ca, dirb, kern0, kern1, kern2, kern3, fits, early, col, rsb, z1b, z2b, agb, scb, spb,
-    in_s, out_s, fit_s, fit_r, rs_s, rs_r, z1_s, z1_r, z2_s, z2_r, ag_s, ag_r, sc_s, sc_r, sp_s, sp_r,
+    xa, ca, dirb, kern0, kern1, kern2, kern3, fits, early, col, rsb, z1b, z2b, zb, agb, scb, spb,
+    in_s, out_s, fit_s, fit_r, rs_s, rs_r, z1_s, z1_r, z2_s, z2_r, z_s, z_r, ag_s, ag_r, sc_s, sc_r, sp_s, sp_r,
 ):
     npts = pts_ref.shape[1]
     tgt, ctrs = dir_ref.shape
@@ -78,7 +81,7 @@
     barrier = pltpu.get_barrier_semaphore()
     peers = [ctr_peer(d) for d in range(1, GROUPS)]
     peers += [plane_peer(d) for d in range(1, PLANE)]
-    peers += [z_peer(d) for d in (3, 6, 9, 1, 11)]
+    peers += [z_peer(d) for d in ALONG_Z]
     for peer in peers:
         pl.semaphore_signal(barrier, inc=1, device_id=peer, device_id_type=MESH)
 
@@ -98,17 +101,17 @@
     loads[1].wait()
     loads[2].wait()
 
-    def centre_block(k, carry):
-        m0 = pl.multiple_of(k * 1024, 1024)
-        c = cen_ref[:, pl.ds(m0, 1024)]
+    def centre_block(k, rows):
+        at = slice(k * rows, (k + 1) * rows)
+        c = cen_ref[:, at]
         c32 = c.astype(F32)
         csq = jnp.sum(c32 * c32, axis=0, keepdims=True) * (-0.125 * LOG2E)
-        tail = tail_rows(1024, three_terms(csq), (1.0, 1.0, 1.0))
-        ca[pl.ds(m0, 1024), :] = jnp.concatenate([c, c, c, tail], axis=0).T
-        dirb[:, pl.ds(m0, 1024)] = dir_ref[:, pl.ds(m0, 1024)].astype(BF16)
-        return carry
-
-    lax.fori_loop(0, ctrs // 1024, centre_block, 0)
+        tail = tail_rows(rows, three_terms(csq), (1.0, 1.0, 1.0))
+        block = jnp.concatenate([c, c, c, tail], axis=0).T
+        ca[at, :] = block
+        dirb[:, at] = dir_ref[:, at].astype(BF16)
+        s = jnp.dot(block, xa[:, :pch], preferred_element_type=F32)
+        kerns[0][at, :] = jnp.exp2(s).astype(BF16)
 
     def fit_copy(i, d):
         return send(
@@ -116,7 +119,10 @@
         )
 
     for i in range(PCH + 1):
-        if i < PCH:
+        if i == 0:
+            for k in range(ctrs // CROWS):
+                centre_block(k, CROWS)
+        elif i < PCH:
             s = jnp.dot(ca[...], xa[:, i * pch : (i + 1) * pch], preferred_element_type=F32)
             kerns[i][...] = jnp.exp2(s).astype(BF16)
         if i > 0:
@@ -151,6 +157,9 @@
             z2b.at[c, step], z2b.at[c, step], z2_s.at[c, d], z2_r.at[c, d], z_peer((1, DEPTH - 1)[d])
         )
 
+    def z_copy(d):
+        return send(zb.at[z], zb.at[z], z_s.at[d], z_r.at[d], z_peer(d))
+
     def ag_copy(c, d):
         return send(
             agb.at[c, mine], agb.at[c, mine], ag_s.at[c, d], ag_r.at[c, d], plane_peer(d)
@@ -170,15 +179,20 @@
     def to_rs(c, part):
         for j in range(PLANE):
             col[c, j] = part[:, j * LANES : (j + 1) * LANES]
-        for d in range(1, PLANE):
+        for d in IN_PLANE:
             rs_copy(c, d).start()
         rsb[c, mine] = col[c, mine]
 
     def to_z1(c):
         for d in range(1, PLANE):
             rs_copy(c, d).wait()
+        if c == MCH - 1:
+            zb[z] = summed(rsb, c, PLANE)
+            for d in ALONG_Z:
+                z_copy(d).start()
+            return
         z1b[c, third] = summed(rsb, c, PLANE)
-        for d in range(1, DEPTH // STRIDE):
+        for d in (2, 1, 3):
             z1_copy(c, d).start()
 
     def to_z2(c):
@@ -191,13 +205,20 @@
     scale = 2048.0 / (npts * DEPTH * PLANE)
 
     def start_ag(c):
-        for d in range(1, PLANE):
+        for d in IN_PLANE:
             ag_copy(c, d).start()
 
     def to_ag(c, sums):
-        for d in range(2):
-            z2_copy(c, d).wait()
-        share = summed(z2b, c, STRIDE)
+        if c == MCH - 1:
+            for d in ALONG_Z:
+                z_copy(d).wait()
+            share = zb[0]
+            for k in range(1, DEPTH):
+                share = share + zb[k]
+        else:
+            for d in range(2):
+                z2_copy(c, d).wait()
+            share = summed(z2b, c, STRIDE)
         agb[c, mine] = share
         if c < MCH - 1:
             start_ag(c)
@@ -229,7 +250,6 @@
     to_z1(3)
     to_z2(2)
     sums = to_ag(1, sums)
-    to_z2(3)
     sums = to_ag(2, sums)
     sums = to_ag(3, sums)
 
@@ -246,7 +266,7 @@
     def sc_copy(d):
         return send(scb.at[ctr], scb.at[ctr], sc_s.at[d], sc_r.at[d], ctr_peer(d))
 
-    for d in range(1, PLANE):
+    for d in IN_PLANE:
         sp_copy(d).start()
     start_ag(MCH - 1)
     for d in range(1, PLANE):
@@ -322,6 +342,7 @@
             pltpu.VMEM((MCH, PLANE, *share), F32),
             pltpu.VMEM((MCH, DEPTH // STRIDE, *share), F32),
             pltpu.VMEM((MCH, STRIDE, *share), F32),
+            pltpu.VMEM((DEPTH, *share), F32),
             pltpu.VMEM((MCH, PLANE, *share), F32),
             pltpu.VMEM((GROUPS, 1, LANES), F32),
             pltpu.VMEM((PLANE, 1, LANES), F32),
@@ -331,6 +352,7 @@
             dma((MCH, PLANE)), dma((MCH, PLANE)),
             dma((MCH, DEPTH // STRIDE)), dma((MCH, DEPTH // STRIDE)),
             dma((MCH, 2)), dma((MCH, 2)),
+            dma((DEPTH,)), dma((DEPTH,)),
             dma((MCH, PLANE)), dma((MCH, PLANE)),
             dma((GROUPS,)), dma((GROUPS,)),
             dma((PLANE,)), dma((PLANE,)),

time: 80.1 us -> 79.3 us (0.990)
  Pallas kernels: 79.3 us -> 78.4 us
    pallas_call x1, Pallas kernels: 76.7 us -> 75.9 us  [shards(): pl.pallas_call(kernel, out_shape=(whole, jax.ShapeDtypeStruct((2, *share)...]
where the time goes in v5:
time: 79.3 us; the launch traced here: 79.1 us
  Pallas kernels  78.4 us (99%)
    pallas_call x1, Pallas kernels, shards(): pl.pallas_call(kernel, out_shape=(whole, jax.ShapeDtypeStruct((2, *share)...  75.9 us
    pallas_call x1, Pallas kernels, shards(): pl.pallas_call(update, out_shape=(whole,) * 3, grid=(UCH,), in_specs=[pl....  2.57 us

profile of v5, /device:TPU:1, one launch (start us, length us, event | category | flops | bytes accessed | tf_op | source)
XLA Modules:
  0.0 79.1 jit_solution(2695379309383125501)
XLA Ops:
  0.6 75.9 %cg_step.1 = (f32[16,8192]{1,0:T(8,128)}, f32[2,16,128]{2,1,0:T(8,128)}) custom-call(bf16[32,2048]{1,0:T(8,128)(2,1)} %pts_hbm.1, bf16[32,8192]{1,0:T(8,128)(2,1)} %cen_hbm.1, f32[16,8192]{1,0:T(8,128)} %dir_ref.1, f32[16,8192]{1,0:T(8,128)} %res_ref.1, f32[1,8192]{1,0:T(1,128)} %bitcast.1), custom_call_target="tpu_custom_call" | custom-call | tf_op jit(solution)/shard_map/cg_step/pallas_call | solution.py:327
  76.5 2.6 %update.1 = (f32[16,8192]{1,0:T(8,128)}, f32[16,8192]{1,0:T(8,128)}, f32[16,8192]{1,0:T(8,128)}) custom-call(f32[2,16,128]{2,1,0:T(8,128)} %get-tuple-element.5.scal_ref, f32[16,8192]{1,0:T(8,128)} %get-tuple-element.6.q_ref, f32[16,8192]{1,0:T(8,128)} %coef_ref.1, f32[16,8192]{1,0:T(8,128)} %res_ref.1, f32[16,8192]{1,0:T(8,128)} %dir_ref.1, f32[1,8192]{1,0:T(1,128)} %bitcast.2), custom_call_target="tpu_custom_call" | custom-call | tf_op jit(solution)/shard_map/update/pallas_call | solution.py:365

commit v6 on v5

--- a/solution.py
+++ b/solution.py
@@ -22,6 +22,7 @@
 EARLY = 2
 UCH = 2
 LANES = 128
+EIGHTHS = (3, 2, 2, 1)
 CROWS = 2048
 IN_PLANE = (4, 12, 3, 5, 11, 13, 2, 6, 10, 14, 1, 7, 9, 15, 8)
 ALONG_Z = (6, 5, 7, 4, 8, 3, 9, 2, 10, 1, 11)
@@ -46,14 +47,16 @@
 def kernel(
     pts_hbm, cen_hbm, dir_hbm, res_hbm, prec_hbm, q_hbm, scal_ref,
     pts_ref, cen_ref, dir_ref, res_ref, prec_ref, q_ref,
-    xa, ca, dirb, kern0, kern1, kern2, kern3, fits, early, col, rsb, z1b, z2b, zb, agb, scb, spb,
+    xa, ca, dirb, kern0, kern1, kern2, kern3, fit0, fit1, fit2, fit3, early, col, rsb, z1b, z2b, zb, agb, scb, spb,
     in_s, out_s, fit_s, fit_r, rs_s, rs_r, z1_s, z1_r, z2_s, z2_r, z_s, z_r, ag_s, ag_r, sc_s, sc_r, sp_s, sp_r,
 ):
     npts = pts_ref.shape[1]
     tgt, ctrs = dir_ref.shape
-    pch = npts // PCH
+    width = [npts // 8 * k for k in EIGHTHS]
+    begin = [sum(width[:k]) for k in range(PCH)]
     mch = ctrs // MCH
     kerns = (kern0, kern1, kern2, kern3)
+    fits = (fit0, fit1, fit2, fit3)
     pts = lax.axis_index("pts")
     ctr = lax.axis_index("ctr")
     z = pts // PLANE
@@ -110,12 +113,12 @@
         block = jnp.concatenate([c, c, c, tail], axis=0).T
         ca[at, :] = block
         dirb[:, at] = dir_ref[:, at].astype(BF16)
-        s = jnp.dot(block, xa[:, :pch], preferred_element_type=F32)
+        s = jnp.dot(block, xa[:, : width[0]], preferred_element_type=F32)
         kerns[0][at, :] = jnp.exp2(s).astype(BF16)
 
     def fit_copy(i, d):
         return send(
-            fits.at[ctr, i], fits.at[ctr, i], fit_s.at[i, d], fit_r.at[i, d], ctr_peer(d)
+            fits[i].at[ctr], fits[i].at[ctr], fit_s.at[i, d], fit_r.at[i, d], ctr_peer(d)
         )
 
     for i in range(PCH + 1):
@@ -123,23 +126,23 @@
             for k in range(ctrs // CROWS):
                 centre_block(k, CROWS)
         elif i < PCH:
-            s = jnp.dot(ca[...], xa[:, i * pch : (i + 1) * pch], preferred_element_type=F32)
+            s = jnp.dot(ca[...], xa[:, begin[i] : begin[i] + width[i]], preferred_element_type=F32)
             kerns[i][...] = jnp.exp2(s).astype(BF16)
         if i > 0:
             part = jnp.dot(dirb[...], kerns[i - 1][...], preferred_element_type=F32)
         if i == 1:
             pl.semaphore_wait(barrier, len(peers))
         if i > 0:
-            fits[ctr, i - 1] = part.astype(BF16)
+            fits[i - 1][ctr] = part.astype(BF16)
             for d in range(1, GROUPS):
                 fit_copy(i - 1, d).start()
 
     def fitted(i):
         for d in range(1, GROUPS):
             fit_copy(i, d).wait()
-        total = fits[0, i].astype(F32)
+        total = fits[i][0].astype(F32)
         for g in range(1, GROUPS):
-            total = total + fits[g, i].astype(F32)
+            total = total + fits[i][g].astype(F32)
         return total.astype(BF16)
 
     def rs_copy(c, d):
@@ -335,8 +338,8 @@
             pltpu.VMEM((128, npts), BF16),
             pltpu.VMEM((ctrs, 128), BF16),
             pltpu.VMEM((tgt, ctrs), BF16),
-            *[pltpu.VMEM((ctrs, npts // PCH), BF16)] * PCH,
-            pltpu.VMEM((GROUPS, PCH, tgt, npts // PCH), BF16),
+            *[pltpu.VMEM((ctrs, npts // 8 * k), BF16) for k in EIGHTHS],
+            *[pltpu.VMEM((GROUPS, tgt, npts // 8 * k), BF16) for k in EIGHTHS],
             pltpu.VMEM((EARLY, tgt, ctrs // MCH), F32),
             pltpu.VMEM((MCH, PLANE, *share), F32),
             pltpu.VMEM((MCH, PLANE, *share), F32),

time: 79.3 us -> 80.8 us (1.019)
  Pallas kernels: 78.4 us -> 79.9 us
    pallas_call x1, Pallas kernels: 75.9 us -> 77.4 us  [shards(): pl.pallas_call(kernel, out_shape=(whole, jax.ShapeDtypeStruct((2, *share)...]
where the time goes in v6:
time: 80.8 us; the launch traced here: 80.6 us
  Pallas kernels  79.9 us (99%)
    pallas_call x1, Pallas kernels, shards(): pl.pallas_call(kernel, out_shape=(whole, jax.ShapeDtypeStruct((2, *share)...  77.4 us
    pallas_call x1, Pallas kernels, shards(): pl.pallas_call(update, out_shape=(whole,) * 3, grid=(UCH,), in_specs=[pl....  2.57 us

profile of v6, /device:TPU:1, one launch (start us, length us, event | category | flops | bytes accessed | tf_op | source)
XLA Modules:
  0.0 80.6 jit_solution(17652556786771250751)
XLA Ops:
  0.6 77.4 %cg_step.1 = (f32[16,8192]{1,0:T(8,128)}, f32[2,16,128]{2,1,0:T(8,128)}) custom-call(bf16[32,2048]{1,0:T(8,128)(2,1)} %pts_hbm.1, bf16[32,8192]{1,0:T(8,128)(2,1)} %cen_hbm.1, f32[16,8192]{1,0:T(8,128)} %dir_ref.1, f32[16,8192]{1,0:T(8,128)} %res_ref.1, f32[1,8192]{1,0:T(1,128)} %bitcast.1), custom_call_target="tpu_custom_call" | custom-call | tf_op jit(solution)/shard_map/cg_step/pallas_call | solution.py:330
  78.0 2.6 %update.1 = (f32[16,8192]{1,0:T(8,128)}, f32[16,8192]{1,0:T(8,128)}, f32[16,8192]{1,0:T(8,128)}) custom-call(f32[2,16,128]{2,1,0:T(8,128)} %get-tuple-element.5.scal_ref, f32[16,8192]{1,0:T(8,128)} %get-tuple-element.6.q_ref, f32[16,8192]{1,0:T(8,128)} %coef_ref.1, f32[16,8192]{1,0:T(8,128)} %res_ref.1, f32[16,8192]{1,0:T(8,128)} %dir_ref.1, f32[1,8192]{1,0:T(1,128)} %bitcast.2), custom_call_target="tpu_custom_call" | custom-call | tf_op jit(solution)/shard_map/update/pallas_call | solution.py:368
